TPU v7x, 128 devices: a whole 4x4x4 slice. The times are simulated.
128 devices in a mesh: dp: 16 (over x, y), owner: 8 (over z, core).
Axes of the slice: x: 4, y: 4, z: 4, core: 2. Of those that a mesh axis runs over, the one named last changes fastest.
Arguments:
- vectors: float32 [96, 262144], P(None, ('dp', 'owner')), as said below
- assignment: int32 [262144], P(('dp', 'owner')), may hold values from 0 to 32767, as said below
- slot: int32 [262144], P(('dp', 'owner')), may hold values from 0 to 15, as said below
- old_centroids: float32 [96, 32768], P(None, ('dp', 'owner')), may hold values from -6 to 6
- prior_counts: int32 [32768], P(('dp', 'owner')), may hold values from 1 to 64
Outputs:
- centroids: float32 [96, 32768], P(None, ('dp', 'owner'))
- rotated: float32 [96, 524288], P(None, ('dp', 'owner'))
Inputs may be any that keep to these rules, and one draw needn't show every extreme that they name: `assignment`: the lists owned by one device are 256 consecutive ones in the order of the devices along dp+owner. Of the 2048 vectors of one device, at most 32 name lists of any one device; in every draw some device receives exactly 32 from every device. No two vectors share a list and a slot; in every draw some list has all 16 slots filled. Finite real vectors.
All inputs are finite; a program needn't handle non-finite values.
Results may differ from a plain program's by a relative error of at most 0.0003.
Values sent between devices are 32-bit elements; how exact they have to be, the bound alone decides.
No kernel may reach another device: no remote copies, remote signals or barrier semaphores. Data moves between devices by JAX's collectives and lax.ppermute only.
A program may use at most 128 MiB of HBM per device.

v0:
```python
import jax
import jax.numpy as jnp
from jax import lax
from jax.experimental import pallas as pl
from jax.experimental.pallas import tpu as pltpu
from jax.sharding import PartitionSpec as P

D = 96
CAP = 16
LISTS = 256
CELLS = LISTS * CAP
TOK = 2048
DEV = 128
SEND = 32
STEPS = 4
AXES = ("dp", "owner")
LANES = 128
TAIL = D - CAP
TOTAL = D * TOK * DEV

shrink_weight = 0.5
epsilon = 1e-05

VMEM = pl.BlockSpec(memory_space=pltpu.VMEM)
BIG = 60 * 1024 * 1024


def dispatch_kernel(vec_ref, assign_ref, slot_ref, send_ref, rows, onehot, pos_v, pos_s, sem):
    f32, bf16, i32 = jnp.float32, jnp.bfloat16, jnp.int32
    chunks = TOK // LANES
    assign = assign_ref[...]
    owner = lax.shift_right_logical(assign, 8)
    here = jnp.bitwise_and(assign, LISTS - 1)
    half = jnp.bitwise_and(here, LANES - 1)
    lane = jnp.bitwise_and(here, LANES) + jnp.bitwise_and(half, 7) * 16 + lax.shift_right_logical(half, 3)
    code = slot_ref[...] * LISTS + lane + 2
    code_high = lax.shift_right_logical(code, 6).astype(f32)
    code_low = jnp.bitwise_and(code, 63).astype(f32)
    sub = lax.broadcasted_iota(i32, (LANES, LANES), 0)
    col = lax.broadcasted_iota(i32, (LANES, LANES), 1)
    for c in range(chunks):
        onehot[c * LANES : (c + 1) * LANES, :] = jnp.where(sub == owner[c : c + 1, :], 1.0, 0.0).astype(bf16)
    before = jnp.concatenate(
        [jnp.where(sub < col, 1.0, 0.0), jnp.ones((LANES, LANES), f32)], axis=1
    ).astype(bf16)
    carry = jnp.zeros((LANES, LANES), f32)
    high = jnp.zeros((LANES, LANES), f32)
    low = jnp.zeros((LANES, LANES), f32)
    lanes_both = (((1,), (1,)), ((), ()))
    for c in range(chunks):
        hot = onehot[c * LANES : (c + 1) * LANES, :]
        counted = jnp.dot(hot, before, preferred_element_type=f32)
        rank = jnp.sum(hot.astype(f32) * (counted[:, :LANES] + carry), axis=0, keepdims=True)
        carry = carry + counted[:, LANES:]
        rank = rank.astype(i32)
        pos_v[c : c + 1, :] = owner[c : c + 1, :] * SEND + rank
        at = sub == rank + D
        high = high + lax.dot_general(
            hot, jnp.where(at, code_high[c : c + 1, :], 0.0).astype(bf16), lanes_both, preferred_element_type=f32
        )
        low = low + lax.dot_general(
            hot, jnp.where(at, code_low[c : c + 1, :], 0.0).astype(bf16), lanes_both, preferred_element_type=f32
        )
    labels = high * 64.0 + low
    labels = jnp.where(labels < 1.0, float(CELLS + 2), labels)
    copy = pltpu.make_async_copy(pos_v, pos_s, sem)
    copy.start()
    fill = jnp.ones((LANES - D, LANES), f32)
    for c in range(chunks):
        block = jnp.concatenate([vec_ref[:, c * LANES : (c + 1) * LANES], fill], axis=0)
        rows[c * LANES : (c + 1) * LANES, :] = block.T
    copy.wait()

    def move(c, carry):
        for t in range(LANES):
            send_ref[pl.ds(pos_s[c, t], 1), :] = rows[pl.ds(c * LANES + t, 1), :]
        return carry

    lax.fori_loop(0, chunks, move, 0)
    lane_row = lax.broadcasted_iota(i32, (1, LANES), 1)
    for d in range(DEV):
        spot = slice(d * SEND, d * SEND + 1)
        send_ref[spot, :] = jnp.where(lane_row >= D, labels[d : d + 1, :], send_ref[spot, :])


def dispatch(vectors, assignment, slot):
    return pl.pallas_call(
        dispatch_kernel,
        out_shape=jax.ShapeDtypeStruct((DEV * SEND, LANES), jnp.float32),
        in_specs=[VMEM] * 3,
        out_specs=VMEM,
        scratch_shapes=[
            pltpu.VMEM((TOK, LANES), jnp.float32),
            pltpu.VMEM((TOK, LANES), jnp.bfloat16),
            pltpu.VMEM((TOK // LANES, LANES), jnp.int32),
            pltpu.SMEM((TOK // LANES, LANES), jnp.int32),
            pltpu.SemaphoreType.DMA,
        ],
        name="dispatch",
    )(vectors, assignment.reshape(TOK // LANES, LANES), slot.reshape(TOK // LANES, LANES))


def place_kernel(got_ref, old_ref, prior_ref, cent_ref, res_ref, stat_ref, energy_ref, cells, lab_v, lab_s, sem):
    f32, i32 = jnp.float32, jnp.int32
    lab_v[...] = got_ref[pl.ds(0, DEV, stride=SEND), :].astype(i32) - 2
    copy = pltpu.make_async_copy(lab_v, lab_s, sem)
    copy.start()
    cells[...] = jnp.zeros(cells.shape, f32)
    copy.wait()

    def move(d, carry):
        for r in range(SEND):
            cells[pl.ds(lab_s[d, D + r], 1), :] = got_ref[pl.ds(d * SEND + r, 1), :]
        return carry

    lax.fori_loop(0, DEV, move, 0)
    lane = lax.broadcasted_iota(i32, (D, LANES), 1)
    to_lane = jnp.bitwise_and(lane, 15) * 8 + lax.shift_right_logical(lane, 4)
    to_list = jnp.bitwise_and(lane, 7) * 16 + lax.shift_right_logical(lane, 3)
    total = jnp.zeros((8, LANES), f32)
    for h in range(LISTS // LANES):
        span = slice(h * LANES, (h + 1) * LANES)
        sums = jnp.zeros((D, LANES), f32)
        counts = jnp.zeros((1, LANES), f32)
        seen = []
        for j in range(CAP):
            start = j * LISTS + h * LANES
            block = cells[start : start + LANES, :].T
            sums = sums + block[:D]
            here = jnp.where(block[D : D + 1] > 0.0, 1.0, 0.0)
            counts = counts + here
            seen.append(here)
            res_ref[j, :, span] = block[:D]
        prior8 = jnp.broadcast_to(prior_ref[:, span].astype(f32), (8, LANES))
        prior = jnp.take_along_axis(prior8, to_lane[:8], axis=1)[:1]
        old = jnp.take_along_axis(old_ref[:, span], to_lane, axis=1)
        weight = prior + counts
        cent = (prior * old + sums) / weight
        cent_ref[:, span] = jnp.take_along_axis(cent, to_list, axis=1)
        stat_ref[:, span] = jnp.concatenate([prior, weight, jnp.zeros((6, LANES), f32)], axis=0)
        for j in range(CAP):
            res = res_ref[j, :, span] - cent * seen[j]
            res_ref[j, :, span] = res
            square = res * res
            for t in range(D // 8):
                total = total + square[8 * t : 8 * t + 8]
    energy_ref[...] = jnp.broadcast_to(jnp.sum(total, axis=0, keepdims=True), (DEV, LANES))


def place(got, old_centroids, prior_counts):
    f32 = jnp.float32
    return pl.pallas_call(
        place_kernel,
        out_shape=(
            jax.ShapeDtypeStruct((D, LISTS), f32),
            jax.ShapeDtypeStruct((CAP, D, LISTS), f32),
            jax.ShapeDtypeStruct((8, LISTS), f32),
            jax.ShapeDtypeStruct((DEV, LANES), f32),
        ),
        in_specs=[VMEM] * 3,
        out_specs=(VMEM,) * 4,
        scratch_shapes=[
            pltpu.VMEM((CELLS + 8, LANES), f32),
            pltpu.VMEM((DEV, LANES), jnp.int32),
            pltpu.SMEM((DEV, LANES), jnp.int32),
            pltpu.SemaphoreType.DMA,
        ],
        name="place",
    )(got, old_centroids, prior_counts.reshape(1, LISTS))


def gram_kernel(res_ref, gram_ref):
    def row(i, carry):
        for h in range(LISTS // LANES):
            span = slice(h * LANES, (h + 1) * LANES)
            left = res_ref[i, :, span]
            for j in range(CAP):
                gram_ref[i, j : j + 1, span] = jnp.sum(left * res_ref[j, :, span], axis=0, keepdims=True)
        return carry

    lax.fori_loop(0, CAP, row, 0)


def gram(res):
    return pl.pallas_call(
        gram_kernel,
        out_shape=jax.ShapeDtypeStruct((CAP, CAP, LISTS), jnp.float32),
        in_specs=[VMEM],
        out_specs=VMEM,
        cost_estimate=pl.CostEstimate(flops=2 * CAP * CAP * D * LISTS, bytes_accessed=4 * CAP * D * LISTS, transcendentals=0),
        name="gram",
    )(res)


def whiten_kernel(res_ref, gram_ref, stat_ref, energy_ref, out_ref, t_ref, m_ref, z_ref, s_ref, o_ref):
    f32, i32 = jnp.float32, jnp.int32
    row_of = lax.broadcasted_iota(i32, (CAP, LISTS), 0)
    energy = jnp.sum(energy_ref[...], axis=(0, 1), keepdims=True)
    shrinkage = shrink_weight * energy / TOTAL + epsilon
    prior = stat_ref[0:1, :]
    weight = stat_ref[1:2, :]
    ridge = shrinkage * prior
    frob = jnp.zeros((CAP, LISTS), f32)
    for i in range(CAP):
        row = (gram_ref[i] + jnp.where(row_of == i, ridge, 0.0)) / weight
        t_ref[i] = row
        frob = frob + row * row
    ridge = ridge / weight
    frob = jnp.sqrt(jnp.sum(frob, axis=0, keepdims=True) + TAIL * (ridge * ridge))

    def times(left, right, into):
        def row(i, carry):
            total = left[i, 0:1, :] * right[0]
            for k in range(1, CAP):
                total = total + left[i, k : k + 1, :] * right[k]
            into[i] = total
            return carry

        lax.fori_loop(0, CAP, row, 0)

    def middle():
        for i in range(CAP):
            m_ref[i] = jnp.where(row_of == i, 1.5, 0.0) - 0.5 * t_ref[i]

    for i in range(CAP):
        t_ref[i] = t_ref[i] / frob
    middle()
    z_ref[...] = m_ref[...]
    for step in range(STEPS - 1):
        times(t_ref, m_ref, s_ref)
        times(s_ref, m_ref, t_ref)
        middle()
        times(m_ref, z_ref, s_ref)
        z_ref[...] = s_ref[...]
    scale = 1.0 / jnp.sqrt(frob)
    for i in range(CAP):
        z_ref[i] = z_ref[i] * scale

    lane = lax.broadcasted_iota(i32, (D, LANES), 1)
    for h in range(LISTS // LANES):
        span = slice(h * LANES, (h + 1) * LANES)

        def apply(j, carry):
            total = res_ref[0, :, span] * z_ref[j, 0:1, span]
            for i in range(1, CAP):
                total = total + res_ref[i, :, span] * z_ref[j, i : i + 1, span]
            o_ref[j] = total
            return carry

        lax.fori_loop(0, CAP, apply, 0)

        def weave(t, carry):
            tile = pl.ds(pl.multiple_of(t * 8, 8), 8)
            parts = [o_ref[j, tile, :] for j in range(CAP)]
            for bit in (8, 4, 2, 1):
                low = jnp.bitwise_and(lane[:8], bit) == 0
                for j in range(CAP):
                    if j & bit == 0:
                        one, two = parts[j], parts[j | bit]
                        parts[j] = jnp.where(low, one, pltpu.roll(two, bit, 1))
                        parts[j | bit] = jnp.where(low, pltpu.roll(one, LANES - bit, 1), two)
            for j in range(CAP):
                at = h * CAP * LANES + j * LANES
                out_ref[tile, at : at + LANES] = parts[j]
            return carry

        lax.fori_loop(0, D // 8, weave, 0)


def whiten(res, gram_blocks, stat, energy):
    f32 = jnp.float32
    return pl.pallas_call(
        whiten_kernel,
        out_shape=jax.ShapeDtypeStruct((D, CELLS), f32),
        in_specs=[VMEM] * 4,
        out_specs=VMEM,
        scratch_shapes=[pltpu.VMEM((CAP, CAP, LISTS), f32)] * 4 + [pltpu.VMEM((CAP, D, LANES), f32)],
        name="whiten",
    )(res, gram_blocks, stat, energy)


def local(vectors, assignment, slot, old_centroids, prior_counts):
    outgoing = dispatch(vectors, assignment, slot).reshape(DEV, SEND, LANES)
    incoming = lax.all_to_all(outgoing, AXES, split_axis=0, concat_axis=0, tiled=True)
    centroids, res, stat, energy = place(incoming.reshape(DEV * SEND, LANES), old_centroids, prior_counts)
    shared = lax.all_to_all(energy.reshape(DEV, 1, LANES), AXES, split_axis=0, concat_axis=0, tiled=True)
    rotated = whiten(res, gram(res), stat, shared.reshape(DEV, LANES))
    return (centroids, rotated)


def solution(mesh):
    placed = (
        P(None, AXES),
        P(AXES),
        P(AXES),
        P(None, AXES),
        P(AXES),
    )
    return jax.shard_map(
        local,
        mesh=mesh,
        in_specs=placed,
        out_specs=(P(None, AXES), P(None, AXES)),
        check_vma=False,
    )
```

profile of v0, /device:TPU:1, one launch (start us, length us, event | category | flops | bytes accessed | tf_op | source)
XLA Modules:
  0.0 92.0 jit_solution(11402159820982135616)
XLA Ops:
  0.6 8.2 %dispatch.1 = f32[4096,128]{1,0:T(8,128)} custom-call(f32[96,2048]{1,0:T(8,128)} %vec_ref.1, s32[16,128]{1,0:T(8,128)} %bitcast.13, s32[16,128]{1,0:T(8,128)} %bitcast.14), custom_call_target="tpu_custom_call" | custom-call | tf_op jit(solution)/shard_map/dispatch/pallas_call | solution.py:87
  8.8 42.0 %all_to_all.10 = f32[128,32,128]{2,1,0:T(8,128)} all-to-all(f32[128,32,128]{2,1,0:T(8,128)} %bitcast.10), channel_id=1, replica_groups=mesh['dp'=16,'owner'=8] {'dp','owner'}, dimensions={0} | all-to-all | bytes 4194304 | tf_op jit(solution)/shard_map/all_to_all | solution.py:284
  50.9 9.5 %place.1 = (f32[96,256]{1,0:T(8,128)}, f32[16,96,256]{2,1,0:T(8,128)}, f32[8,256]{1,0:T(8,128)}, f32[128,128]{1,0:T(8,128)}) custom-call(f32[4096,128]{1,0:T(8,128)} %bitcast.9, f32[96,256]{1,0:T(8,128)} %old_ref.1, s32[1,256]{1,0:T(1,128)} %bitcast.15), custom_call_target="tpu_custom_call" | custom-call | tf_op jit(solution)/shard_map/place/pallas_call | solution.py:152
  60.4 4.6 %all-to-all-start.1 = ((f32[128,1,128]{2,1,0:T(1,128)}), f32[128,1,128]{2,1,0:T(1,128)S(1)}, u32[]{:S(2)}, u32[]{:S(2)}) async-start(f32[128,1,128]{2,1,0:T(1,128)} %bitcast.12), calls=%async_computation.1 | async-start | bytes 131072 | tf_op jit(solution)/shard_map/all_to_all | solution.py:286
  65.0 4.3 %gram.1.gram_ref = f32[16,16,256]{2,1,0:T(8,128)} custom-call(f32[16,96,256]{2,1,0:T(8,128)} %get-tuple-element.7.res_ref), custom_call_target="tpu_custom_call" | custom-call | flops 12582912 | bytes 1572864 | tf_op jit(solution)/shard_map/gram/pallas_call | solution.py:185
  69.3 5.1 %all-to-all-done.1 = f32[128,1,128]{2,1,0:T(1,128)S(1)} async-done(((f32[128,1,128]{2,1,0:T(1,128)}), f32[128,1,128]{2,1,0:T(1,128)S(1)}, u32[]{:S(2)}, u32[]{:S(2)}) %all-to-all-start.1) | async-done | bytes 65568 | tf_op jit(solution)/shard_map/all_to_all | solution.py:286
  74.4 0.0 copy-start
  74.4 0.6 copy-done
  75.1 16.9 %whiten.1 = f32[96,4096]{1,0:T(8,128)} custom-call(f32[16,96,256]{2,1,0:T(8,128)} %get-tuple-element.7.res_ref, f32[16,16,256]{2,1,0:T(8,128)} %gram.1.gram_ref, f32[8,256]{1,0:T(8,128)} %get-tuple-element.8.stat_ref, f32[128,128]{1,0:T(8,128)} %bitcast.11), custom_call_target="tpu_custom_call" | custom-call | tf_op jit(solution)/shard_map/whiten/pallas_call | solution.py:272
Async XLA Ops:
  60.4 14.1 %all-to-all-start.1 = ((f32[128,1,128]{2,1,0:T(1,128)}), f32[128,1,128]{2,1,0:T(1,128)S(1)}, u32[]{:S(2)}, u32[]{:S(2)}) async-start(f32[128,1,128]{2,1,0:T(1,128)} %bitcast.12), calls=%async_computation.1 | async-start | bytes 131072 | tf_op jit(solution)/shard_map/all_to_all | solution.py:286
  74.4 0.6 copy-start
where the time goes:
time: 92.3 us; the launch traced here: 92 us
  blocking collectives  42 us (46%)
  Pallas kernels  38.9 us (42%)
  waiting for transfers between devices  5.13 us (6%)
  starting transfers between devices  4.62 us (5%)
    all_to_all x1, blocking collectives, local(): lax.all_to_all(outgoing, AXES, split_axis=0, concat_axis=0, tiled=True)  42 us
    pallas_call x1, Pallas kernels, whiten(): pl.pallas_call(whiten_kernel, out_shape=jax.ShapeDtypeStruct((D, CELLS),...  16.9 us
    pallas_call x1, Pallas kernels, place(): pl.pallas_call(place_kernel, out_shape=(jax.ShapeDtypeStruct((D, LISTS),...  9.47 us
    pallas_call x1, Pallas kernels, dispatch(): pl.pallas_call(dispatch_kernel, out_shape=jax.ShapeDtypeStruct((DEV * SEN...  8.21 us
    all_to_all x1, waiting for transfers between devices, local(): lax.all_to_all(energy.reshape(DEV, 1, LANES), AXES, split_axis=0, concat_...  5.13 us
    all_to_all x1, starting transfers between devices, local(): lax.all_to_all(energy.reshape(DEV, 1, LANES), AXES, split_axis=0, concat_...  4.62 us
    pallas_call x1, Pallas kernels, gram(): pl.pallas_call(gram_kernel, out_shape=jax.ShapeDtypeStruct((CAP, CAP, LIS...  4.32 us
  transfers between devices with their start and end apart: 1, of which 1 were waited for; matrix products, arithmetic and copies ran while one was open for 0% of the time, Pallas kernels for 5%

commit v1 on v0

v1 whole, which is shorter than its diff:
```python
import jax
import jax.numpy as jnp
from jax import lax
from jax.experimental import pallas as pl
from jax.experimental.pallas import tpu as pltpu
from jax.sharding import PartitionSpec as P

D = 96
CAP = 16
LISTS = 256
CELLS = LISTS * CAP
TOK = 2048
DEV = 128
SEND = 32
STEPS = 4
AXES = ("dp", "owner")
LANES = 128
TAIL = D - CAP
MAIN = 24
BLOCK = MAIN + 1
TOTAL = D * TOK * DEV

shrink_weight = 0.5
epsilon = 1e-05

VMEM = pl.BlockSpec(memory_space=pltpu.VMEM)
BIG = 60 * 1024 * 1024


def dispatch_kernel(vec_ref, assign_ref, slot_ref, send_ref, rows, stage, pos_v, pos_s, sem):
    f32, bf16, i32 = jnp.float32, jnp.bfloat16, jnp.int32
    wide = 2 * LANES
    assign = assign_ref[...]
    owner = lax.shift_right_logical(assign, 8)
    here = jnp.bitwise_and(assign, LISTS - 1)
    half = jnp.bitwise_and(here, LANES - 1)
    lane = jnp.bitwise_and(here, LANES) + jnp.bitwise_and(half, 7) * 16 + lax.shift_right_logical(half, 3)
    code = slot_ref[...] * LISTS + lane + 1
    code_high = lax.shift_right_logical(code, 6).astype(f32)
    code_low = jnp.bitwise_and(code, 63).astype(f32)

    def pair(x, c):
        return jnp.concatenate([x[2 * c : 2 * c + 1, :], x[2 * c + 1 : 2 * c + 2, :]], axis=1)

    sub = lax.broadcasted_iota(i32, (LANES, wide), 0)
    slots = lax.broadcasted_iota(i32, (SEND, wide), 0)
    row2 = lax.broadcasted_iota(i32, (wide, wide), 0)
    col2 = lax.broadcasted_iota(i32, (wide, wide), 1)
    before = jnp.concatenate([jnp.where(row2 < col2, 1.0, 0.0), jnp.ones((wide, wide), f32)], axis=1).astype(bf16)
    carry = jnp.zeros((LANES, wide), f32)
    codes = jnp.zeros((LANES, 2 * SEND), f32)
    for c in range(TOK // wide):
        mine = pair(owner, c)
        picked = sub == mine
        hot = jnp.where(picked, 1.0, 0.0).astype(bf16)
        counted = jnp.dot(hot, before, preferred_element_type=f32)
        rank = jnp.sum(jnp.where(picked, counted[:, :wide] + carry, 0.0), axis=0, keepdims=True).astype(i32)
        carry = carry + counted[:, wide:]
        pos = jnp.where(rank < MAIN, mine * BLOCK + rank, DEV * BLOCK - MAIN + mine * (SEND - MAIN) + rank)
        pos_v[2 * c : 2 * c + 1, :] = pos[:, :LANES]
        pos_v[2 * c + 1 : 2 * c + 2, :] = pos[:, LANES:]
        at = slots == rank
        marks = jnp.concatenate(
            [jnp.where(at, pair(code_high, c), 0.0), jnp.where(at, pair(code_low, c), 0.0)], axis=0
        ).astype(bf16)
        codes = codes + lax.dot_general(hot, marks, (((1,), (1,)), ((), ())), preferred_element_type=f32)
    copy = pltpu.make_async_copy(pos_v, pos_s, sem)
    copy.start()
    labels = codes[:, :SEND] * 64.0 + codes[:, SEND:] - 1.0
    labels = jnp.where(labels < 0.0, float(CELLS), labels)
    labels = jnp.concatenate([labels, jnp.zeros((DEV, LANES - SEND), f32)], axis=1)
    send_ref[pl.ds(MAIN, DEV, stride=BLOCK), :] = labels
    fill = jnp.zeros((LANES - D, LANES), f32)
    for c in range(TOK // LANES):
        block = jnp.concatenate([vec_ref[:, c * LANES : (c + 1) * LANES], fill], axis=0)
        rows[c * LANES : (c + 1) * LANES, :] = block.T
    copy.wait()
    for c in range(TOK // LANES):
        for t in range(LANES):
            stage[pl.ds(pos_s[c, t], 1), :] = rows[c * LANES + t : c * LANES + t + 1, :]
    outer = lax.broadcasted_iota(i32, (8, LANES), 1) >= D

    def pack(d, carry):
        tail = stage[pl.ds(pl.multiple_of(DEV * BLOCK + 8 * d, 8), 8), :]
        for k in range(MAIN // 8):
            spot = pl.ds(d * BLOCK + 8 * k, 8)
            send_ref[spot, :] = jnp.where(outer, pltpu.roll(tail, D - 32 * k, 1), stage[spot, :])
        return carry

    lax.fori_loop(0, DEV, pack, 0, unroll=8)


def dispatch(vectors, assignment, slot):
    return pl.pallas_call(
        dispatch_kernel,
        out_shape=jax.ShapeDtypeStruct((DEV * BLOCK, LANES), jnp.float32),
        in_specs=[VMEM] * 3,
        out_specs=VMEM,
        scratch_shapes=[
            pltpu.VMEM((TOK, LANES), jnp.float32),
            pltpu.VMEM((DEV * (BLOCK + SEND - MAIN), LANES), jnp.float32),
            pltpu.VMEM((TOK // LANES, LANES), jnp.int32),
            pltpu.SMEM((TOK // LANES, LANES), jnp.int32),
            pltpu.SemaphoreType.DMA,
        ],
        name="dispatch",
    )(vectors, assignment.reshape(TOK // LANES, LANES), slot.reshape(TOK // LANES, LANES))


def place_kernel(got_ref, old_ref, prior_ref, cent_ref, res_ref, stat_ref, energy_ref, cells, tails, lab_v, lab_s, sem):
    f32, i32 = jnp.float32, jnp.int32
    lab_v[...] = got_ref[pl.ds(MAIN, DEV, stride=BLOCK), :].astype(i32)
    copy = pltpu.make_async_copy(lab_v, lab_s, sem)
    copy.start()
    cells[...] = jnp.full(cells.shape, jnp.inf, f32)
    near = lax.broadcasted_iota(i32, (8, LANES), 1)

    def unpack(d, carry):
        first, second, third = (
            pltpu.roll(got_ref[pl.ds(d * BLOCK + 8 * k, 8), :], 32 * k + 32, 1) for k in range(MAIN // 8)
        )
        tail = jnp.where(near < 32, first, jnp.where(near < 64, second, third))
        tails[pl.ds(pl.multiple_of(8 * d, 8), 8), :] = tail
        return carry

    lax.fori_loop(0, DEV, unpack, 0, unroll=8)
    copy.wait()
    for d in range(DEV):
        for r in range(MAIN):
            cells[pl.ds(lab_s[d, r], 1), :] = got_ref[d * BLOCK + r : d * BLOCK + r + 1, :]
        for r in range(MAIN, SEND):
            spot = d * (SEND - MAIN) + r - MAIN
            cells[pl.ds(lab_s[d, r], 1), :] = tails[spot : spot + 1, :]
    lane = lax.broadcasted_iota(i32, (D, LANES), 1)
    to_lane = jnp.bitwise_and(lane, 15) * 8 + lax.shift_right_logical(lane, 4)
    to_list = jnp.bitwise_and(lane, 7) * 16 + lax.shift_right_logical(lane, 3)
    total = jnp.zeros((8, LANES), f32)
    for h in range(LISTS // LANES):
        span = slice(h * LANES, (h + 1) * LANES)
        sums = jnp.zeros((D, LANES), f32)
        counts = jnp.zeros((1, LANES), f32)
        seen = []
        for j in range(CAP):
            start = j * LISTS + h * LANES
            block = cells[start : start + LANES, :].T[:D]
            full = block[:1] < jnp.inf
            block = jnp.where(full, block, 0.0)
            here = jnp.where(full, 1.0, 0.0)
            sums = sums + block
            counts = counts + here
            seen.append(here)
            res_ref[j, :, span] = block
        prior8 = jnp.broadcast_to(prior_ref[:, span].astype(f32), (8, LANES))
        prior = jnp.take_along_axis(prior8, to_lane[:8], axis=1)[:1]
        old = jnp.take_along_axis(old_ref[:, span], to_lane, axis=1)
        weight = prior + counts
        cent = (prior * old + sums) / weight
        cent_ref[:, span] = jnp.take_along_axis(cent, to_list, axis=1)
        stat_ref[:, span] = jnp.concatenate([prior, weight, jnp.zeros((6, LANES), f32)], axis=0)
        for j in range(CAP):
            res = res_ref[j, :, span] - cent * seen[j]
            res_ref[j, :, span] = res
            square = res * res
            for t in range(D // 8):
                total = total + square[8 * t : 8 * t + 8]
    energy_ref[...] = jnp.broadcast_to(jnp.sum(total, axis=0, keepdims=True), (DEV, LANES))


def place(got, old_centroids, prior_counts):
    f32 = jnp.float32
    return pl.pallas_call(
        place_kernel,
        out_shape=(
            jax.ShapeDtypeStruct((D, LISTS), f32),
            jax.ShapeDtypeStruct((CAP, D, LISTS), f32),
            jax.ShapeDtypeStruct((8, LISTS), f32),
            jax.ShapeDtypeStruct((DEV, LANES), f32),
        ),
        in_specs=[VMEM] * 3,
        out_specs=(VMEM,) * 4,
        scratch_shapes=[
            pltpu.VMEM((CELLS + 8, LANES), f32),
            pltpu.VMEM((DEV * (SEND - MAIN), LANES), f32),
            pltpu.VMEM((DEV, LANES), jnp.int32),
            pltpu.SMEM((DEV, LANES), jnp.int32),
            pltpu.SemaphoreType.DMA,
        ],
        name="place",
    )(got, old_centroids, prior_counts.reshape(1, LISTS))


def gram_kernel(res_ref, gram_ref):
    def row(i, carry):
        for h in range(LISTS // LANES):
            span = slice(h * LANES, (h + 1) * LANES)
            left = res_ref[i, :, span]
            for step in range(CAP // 2 + 1):
                j = jnp.bitwise_and(i + step, CAP - 1)
                value = jnp.sum(left * res_ref[j, :, span], axis=0, keepdims=True)
                gram_ref[h, i, pl.ds(j, 1), :] = value
                gram_ref[h, j, pl.ds(i, 1), :] = value
        return carry

    lax.fori_loop(0, CAP, row, 0)


def gram(res):
    return pl.pallas_call(
        gram_kernel,
        out_shape=jax.ShapeDtypeStruct((LISTS // LANES, CAP, CAP, LANES), jnp.float32),
        in_specs=[VMEM],
        out_specs=VMEM,
        cost_estimate=pl.CostEstimate(flops=2 * CAP * CAP * D * LISTS, bytes_accessed=4 * CAP * D * LISTS, transcendentals=0),
        name="gram",
    )(res)


def whiten_kernel(res_ref, gram_ref, stat_ref, energy_ref, out_ref, t_ref, z_ref, s_ref, q_ref, o_ref):
    f32, i32 = jnp.float32, jnp.int32
    group = 4
    row_of = lax.broadcasted_iota(i32, (CAP, LANES), 0)
    energy = jnp.sum(energy_ref[...], axis=(0, 1), keepdims=True)
    shrinkage = shrink_weight * energy / TOTAL + epsilon
    for h in range(LISTS // LANES):
        span = slice(h * LANES, (h + 1) * LANES)
        weight = stat_ref[1:2, span]
        share = 1.0 / weight
        ridge = shrinkage * stat_ref[0:1, span]
        frob = jnp.zeros((CAP, LANES), f32)
        for i in range(CAP):
            row = (gram_ref[h, i] + jnp.where(row_of == i, ridge, 0.0)) * share
            t_ref[i] = row
            frob = frob + row * row
        ridge = ridge * share
        frob = jnp.sqrt(jnp.sum(frob, axis=0, keepdims=True) + TAIL * (ridge * ridge))
        scale = 1.0 / frob
        middle = []
        for i in range(CAP):
            row = t_ref[i] * scale
            t_ref[i] = row
            middle.append(jnp.where(row_of == i, 1.5, 0.0) - 0.5 * row)
            z_ref[i] = middle[i]

        def times(left, i, middle):
            total = left[i, 0:1, :] * middle[0]
            for k in range(1, CAP):
                total = total + left[i, k : k + 1, :] * middle[k]
            return total

        for step in range(STEPS):

            def advance(block, carry, step=step, middle=middle):
                spots = [block * group + g for g in range(group)]
                if step < STEPS - 1:
                    for i in spots:
                        s_ref[i] = times(t_ref, i, middle)
                if step > 0:
                    for i in spots:
                        moved = times(z_ref, i, middle)
                        if step == STEPS - 1:
                            q_ref[h, i] = moved * root
                        else:
                            z_ref[i] = moved
                if step < STEPS - 1:
                    for i in spots:
                        t_ref[i] = times(s_ref, i, middle)
                return carry

            root = 1.0 / jnp.sqrt(frob)
            lax.fori_loop(0, CAP // group, advance, 0)
            if step < STEPS - 1:
                middle = [jnp.where(row_of == i, 1.5, 0.0) - 0.5 * t_ref[i] for i in range(CAP)]

    lane = lax.broadcasted_iota(i32, (8, LANES), 1)
    tiles = D // 8

    def weave(n):
        parts = [o_ref[j] for j in range(CAP)]

        def finish():
            h, t = n // tiles, n % tiles
            for bit in (8, 4, 2, 1):
                low = jnp.bitwise_and(lane, bit) == 0
                for j in range(CAP):
                    if j & bit == 0:
                        one, two = parts[j], parts[j | bit]
                        parts[j] = jnp.where(low, one, pltpu.roll(two, bit, 1))
                        parts[j | bit] = jnp.where(low, pltpu.roll(one, LANES - bit, 1), two)
            for j in range(CAP):
                at = pl.multiple_of(h * (CAP * LANES) + j * LANES, LANES)
                out_ref[pl.ds(pl.multiple_of(t * 8, 8), 8), pl.ds(at, LANES)] = parts[j]

        return finish

    def apply(n, carry):
        finish = weave(jnp.maximum(n - 1, 0))
        h, t = n // tiles, n % tiles
        tile = pl.ds(pl.multiple_of(t * 8, 8), 8)
        span = pl.ds(pl.multiple_of(h * LANES, LANES), LANES)
        pieces = [res_ref[i, tile, span] for i in range(CAP)]
        for j in range(CAP):
            total = pieces[0] * q_ref[h, j, 0:1, :]
            for i in range(1, CAP):
                total = total + pieces[i] * q_ref[h, j, i : i + 1, :]
            o_ref[j] = total
        finish()
        return carry

    last = tiles * (LISTS // LANES)
    lax.fori_loop(0, last, apply, 0)
    weave(last - 1)()


def whiten(res, gram_blocks, stat, energy):
    f32 = jnp.float32
    return pl.pallas_call(
        whiten_kernel,
        out_shape=jax.ShapeDtypeStruct((D, CELLS), f32),
        in_specs=[VMEM] * 4,
        out_specs=VMEM,
        scratch_shapes=[pltpu.VMEM((CAP, CAP, LANES), f32)] * 3
        + [pltpu.VMEM((LISTS // LANES, CAP, CAP, LANES), f32), pltpu.VMEM((CAP, 8, LANES), f32)],
        name="whiten",
    )(res, gram_blocks, stat, energy)


def local(vectors, assignment, slot, old_centroids, prior_counts):
    outgoing = dispatch(vectors, assignment, slot).reshape(DEV, 1, BLOCK * LANES)
    incoming = lax.all_to_all(outgoing, AXES, split_axis=0, concat_axis=0, tiled=True)
    centroids, res, stat, energy = place(incoming.reshape(DEV * BLOCK, LANES), old_centroids, prior_counts)
    shared = lax.all_to_all(energy.reshape(DEV, 1, LANES), AXES, split_axis=0, concat_axis=0, tiled=True)
    rotated = whiten(res, gram(res), stat, shared.reshape(DEV, LANES))
    return (centroids, rotated)


def solution(mesh):
    placed = (
        P(None, AXES),
        P(AXES),
        P(AXES),
        P(None, AXES),
        P(AXES),
    )
    return jax.shard_map(
        local,
        mesh=mesh,
        in_specs=placed,
        out_specs=(P(None, AXES), P(None, AXES)),
        check_vma=False,
    )
```

time: 92.3 us -> 79.4 us (0.86)
  Pallas kernels: 38.9 us -> 30.2 us
  blocking collectives: 42 us -> 37.1 us
    all_to_all x1, blocking collectives: 42 us -> 37.1 us  [local(): lax.all_to_all(outgoing, AXES, split_axis=0, concat_axis=0, tiled=True)]
    pallas_call x1, Pallas kernels: 16.9 us -> 12.9 us  [whiten(): pl.pallas_call(whiten_kernel, out_shape=jax.ShapeDtypeStruct((D, CELLS),...]
    pallas_call x2, Pallas kernels: 12.5 us -> 9.92 us  [the longest x1 6.35 us: dispatch(): pl.pallas_call(dispatch_kernel, out_shape=jax.ShapeDtypeStruct((DEV * BLO...]
    pallas_call x1, Pallas kernels: 9.47 us -> 7.35 us  [place(): pl.pallas_call(place_kernel, out_shape=(jax.ShapeDtypeStruct((D, LISTS),...]
where the time goes in v1:
time: 79.4 us; the launch traced here: 79.1 us
  blocking collectives  37.1 us (47%)
  Pallas kernels  30.2 us (38%)
  waiting for transfers between devices  5.87 us (7%)
  starting transfers between devices  4.63 us (6%)
    all_to_all x1, blocking collectives, local(): lax.all_to_all(outgoing, AXES, split_axis=0, concat_axis=0, tiled=True)  37.1 us
    pallas_call x1, Pallas kernels, whiten(): pl.pallas_call(whiten_kernel, out_shape=jax.ShapeDtypeStruct((D, CELLS),...  12.9 us
    pallas_call x1, Pallas kernels, place(): pl.pallas_call(place_kernel, out_shape=(jax.ShapeDtypeStruct((D, LISTS),...  7.35 us
    pallas_call x1, Pallas kernels, dispatch(): pl.pallas_call(dispatch_kernel, out_shape=jax.ShapeDtypeStruct((DEV * BLO...  6.35 us
    all_to_all x1, waiting for transfers between devices, local(): lax.all_to_all(energy.reshape(DEV, 1, LANES), AXES, split_axis=0, concat_...  5.87 us
    all_to_all x1, starting transfers between devices, local(): lax.all_to_all(energy.reshape(DEV, 1, LANES), AXES, split_axis=0, concat_...  4.63 us
    pallas_call x1, Pallas kernels, gram(): pl.pallas_call(gram_kernel, out_shape=jax.ShapeDtypeStruct((LISTS // LANE...  3.58 us
  transfers between devices with their start and end apart: 1, of which 1 were waited for; matrix products, arithmetic and copies ran while one was open for 0% of the time, Pallas kernels for 5%

profile of v1, /device:TPU:1, one launch (start us, length us, event | category | flops | bytes accessed | tf_op | source)
XLA Modules:
  0.0 79.1 jit_solution(2255340777973316949)
XLA Ops:
  0.6 6.3 %dispatch.1 = f32[3200,128]{1,0:T(8,128)} custom-call(f32[96,2048]{1,0:T(8,128)} %vec_ref.1, s32[16,128]{1,0:T(8,128)} %bitcast.13, s32[16,128]{1,0:T(8,128)} %bitcast.14), custom_call_target="tpu_custom_call" | custom-call | tf_op jit(solution)/shard_map/dispatch/pallas_call | solution.py:94
  7.0 37.1 %all_to_all.10 = f32[128,1,3200]{2,1,0:T(1,128)} all-to-all(f32[128,1,3200]{2,1,0:T(1,128)} %bitcast.10), channel_id=1, replica_groups=mesh['dp'=16,'owner'=8] {'dp','owner'}, dimensions={0} | all-to-all | bytes 3276800 | tf_op jit(solution)/shard_map/all_to_all | solution.py:329
  44.1 7.4 %place.1 = (f32[96,256]{1,0:T(8,128)}, f32[16,96,256]{2,1,0:T(8,128)}, f32[8,256]{1,0:T(8,128)}, f32[128,128]{1,0:T(8,128)}) custom-call(f32[3200,128]{1,0:T(8,128)} %bitcast.9, f32[96,256]{1,0:T(8,128)} %old_ref.1, s32[1,256]{1,0:T(1,128)} %bitcast.15), custom_call_target="tpu_custom_call" | custom-call | tf_op jit(solution)/shard_map/place/pallas_call | solution.py:171
  51.5 4.6 %all-to-all-start.1 = ((f32[128,1,128]{2,1,0:T(1,128)}), f32[128,1,128]{2,1,0:T(1,128)S(1)}, u32[]{:S(2)}, u32[]{:S(2)}) async-start(f32[128,1,128]{2,1,0:T(1,128)} %bitcast.12), calls=%async_computation.1 | async-start | bytes 131072 | tf_op jit(solution)/shard_map/all_to_all | solution.py:331
  56.1 3.6 %gram.1.gram_ref = f32[2,16,16,128]{3,2,1,0:T(8,128)} custom-call(f32[16,96,256]{2,1,0:T(8,128)} %get-tuple-element.7.res_ref), custom_call_target="tpu_custom_call" | custom-call | flops 12582912 | bytes 1572864 | tf_op jit(solution)/shard_map/gram/pallas_call | solution.py:208
  59.7 5.9 %all-to-all-done.1 = f32[128,1,128]{2,1,0:T(1,128)S(1)} async-done(((f32[128,1,128]{2,1,0:T(1,128)}), f32[128,1,128]{2,1,0:T(1,128)S(1)}, u32[]{:S(2)}, u32[]{:S(2)}) %all-to-all-start.1) | async-done | bytes 65568 | tf_op jit(solution)/shard_map/all_to_all | solution.py:331
  65.5 0.0 copy-start
  65.5 0.6 copy-done
  66.2 12.9 %whiten.1 = f32[96,4096]{1,0:T(8,128)} custom-call(f32[16,96,256]{2,1,0:T(8,128)} %get-tuple-element.7.res_ref, f32[2,16,16,128]{3,2,1,0:T(8,128)} %gram.1.gram_ref, f32[8,256]{1,0:T(8,128)} %get-tuple-element.8.stat_ref, f32[128,128]{1,0:T(8,128)} %bitcast.11), custom_call_target="tpu_custom_call" | custom-call | tf_op jit(solution)/shard_map/whiten/pallas_call | solution.py:316
Async XLA Ops:
  51.5 14.1 %all-to-all-start.1 = ((f32[128,1,128]{2,1,0:T(1,128)}), f32[128,1,128]{2,1,0:T(1,128)S(1)}, u32[]{:S(2)}, u32[]{:S(2)}) async-start(f32[128,1,128]{2,1,0:T(1,128)} %bitcast.12), calls=%async_computation.1 | async-start | bytes 131072 | tf_op jit(solution)/shard_map/all_to_all | solution.py:331
  65.5 0.6 copy-start

commit v2 on v1

--- a/solution.py
+++ b/solution.py
@@ -24,12 +24,20 @@
 epsilon = 1e-05
 
 VMEM = pl.BlockSpec(memory_space=pltpu.VMEM)
-BIG = 60 * 1024 * 1024
-
-
-def dispatch_kernel(vec_ref, assign_ref, slot_ref, send_ref, rows, stage, pos_v, pos_s, sem):
+GRANT = 16 * 1024 * 1024
+
+
+def dispatch_kernel(vec_hbm, assign_hbm, slot_hbm, send_ref, vec_ref, assign_ref, slot_ref, rows, stage, pos_v, pos_s, sem):
     f32, bf16, i32 = jnp.float32, jnp.bfloat16, jnp.int32
     wide = 2 * LANES
+    get_assign = pltpu.make_async_copy(assign_hbm, assign_ref, sem.at[0])
+    get_slot = pltpu.make_async_copy(slot_hbm, slot_ref, sem.at[1])
+    get_vectors = pltpu.make_async_copy(vec_hbm, vec_ref, sem.at[2])
+    get_assign.start()
+    get_slot.start()
+    get_vectors.start()
+    get_assign.wait()
+    get_slot.wait()
     assign = assign_ref[...]
     owner = lax.shift_right_logical(assign, 8)
     here = jnp.bitwise_and(assign, LISTS - 1)
@@ -64,20 +72,24 @@
             [jnp.where(at, pair(code_high, c), 0.0), jnp.where(at, pair(code_low, c), 0.0)], axis=0
         ).astype(bf16)
         codes = codes + lax.dot_general(hot, marks, (((1,), (1,)), ((), ())), preferred_element_type=f32)
-    copy = pltpu.make_async_copy(pos_v, pos_s, sem)
+    copy = pltpu.make_async_copy(pos_v, pos_s, sem.at[3])
     copy.start()
     labels = codes[:, :SEND] * 64.0 + codes[:, SEND:] - 1.0
     labels = jnp.where(labels < 0.0, float(CELLS), labels)
     labels = jnp.concatenate([labels, jnp.zeros((DEV, LANES - SEND), f32)], axis=1)
     send_ref[pl.ds(MAIN, DEV, stride=BLOCK), :] = labels
     fill = jnp.zeros((LANES - D, LANES), f32)
+    get_vectors.wait()
     for c in range(TOK // LANES):
         block = jnp.concatenate([vec_ref[:, c * LANES : (c + 1) * LANES], fill], axis=0)
         rows[c * LANES : (c + 1) * LANES, :] = block.T
     copy.wait()
-    for c in range(TOK // LANES):
-        for t in range(LANES):
-            stage[pl.ds(pos_s[c, t], 1), :] = rows[c * LANES + t : c * LANES + t + 1, :]
+
+    def move(t, carry):
+        stage[pl.ds(pos_s[t // LANES, t % LANES], 1), :] = rows[pl.ds(t, 1), :]
+        return carry
+
+    lax.fori_loop(0, TOK, move, 0, unroll=True)
     outer = lax.broadcasted_iota(i32, (8, LANES), 1) >= D
 
     def pack(d, carry):
@@ -91,23 +103,28 @@
 
 
 def dispatch(vectors, assignment, slot):
+    arrays = (vectors, assignment.reshape(TOK // LANES, LANES), slot.reshape(TOK // LANES, LANES))
     return pl.pallas_call(
         dispatch_kernel,
         out_shape=jax.ShapeDtypeStruct((DEV * BLOCK, LANES), jnp.float32),
-        in_specs=[VMEM] * 3,
+        in_specs=[pl.BlockSpec(memory_space=pltpu.HBM)] * 3,
         out_specs=VMEM,
         scratch_shapes=[
+            pltpu.VMEM((D, TOK), jnp.float32),
+            pltpu.VMEM((TOK // LANES, LANES), jnp.int32),
+            pltpu.VMEM((TOK // LANES, LANES), jnp.int32),
             pltpu.VMEM((TOK, LANES), jnp.float32),
             pltpu.VMEM((DEV * (BLOCK + SEND - MAIN), LANES), jnp.float32),
             pltpu.VMEM((TOK // LANES, LANES), jnp.int32),
             pltpu.SMEM((TOK // LANES, LANES), jnp.int32),
-            pltpu.SemaphoreType.DMA,
+            pltpu.SemaphoreType.DMA((4,)),
         ],
+        compiler_params=pltpu.CompilerParams(vmem_limit_bytes=GRANT),
         name="dispatch",
-    )(vectors, assignment.reshape(TOK // LANES, LANES), slot.reshape(TOK // LANES, LANES))
-
-
-def place_kernel(got_ref, old_ref, prior_ref, cent_ref, res_ref, stat_ref, energy_ref, cells, tails, lab_v, lab_s, sem):
+    )(*(pltpu.with_memory_space_constraint(x, pltpu.HBM) for x in arrays))
+
+
+def place_kernel(got_ref, old_ref, prior_ref, res_ref, stat_ref, energy_ref, cells, tails, lab_v, lab_s, sem):
     f32, i32 = jnp.float32, jnp.int32
     lab_v[...] = got_ref[pl.ds(MAIN, DEV, stride=BLOCK), :].astype(i32)
     copy = pltpu.make_async_copy(lab_v, lab_s, sem)
@@ -125,15 +142,18 @@
 
     lax.fori_loop(0, DEV, unpack, 0, unroll=8)
     copy.wait()
-    for d in range(DEV):
+
+    def move(d, carry):
+        labels = lab_s.at[d]
         for r in range(MAIN):
-            cells[pl.ds(lab_s[d, r], 1), :] = got_ref[d * BLOCK + r : d * BLOCK + r + 1, :]
+            cells[pl.ds(labels[r], 1), :] = got_ref[pl.ds(d * BLOCK + r, 1), :]
         for r in range(MAIN, SEND):
-            spot = d * (SEND - MAIN) + r - MAIN
-            cells[pl.ds(lab_s[d, r], 1), :] = tails[spot : spot + 1, :]
+            cells[pl.ds(labels[r], 1), :] = tails[pl.ds(d * (SEND - MAIN) + r - MAIN, 1), :]
+        return carry
+
+    lax.fori_loop(0, DEV, move, 0, unroll=True)
     lane = lax.broadcasted_iota(i32, (D, LANES), 1)
     to_lane = jnp.bitwise_and(lane, 15) * 8 + lax.shift_right_logical(lane, 4)
-    to_list = jnp.bitwise_and(lane, 7) * 16 + lax.shift_right_logical(lane, 3)
     total = jnp.zeros((8, LANES), f32)
     for h in range(LISTS // LANES):
         span = slice(h * LANES, (h + 1) * LANES)
@@ -155,7 +175,7 @@
         old = jnp.take_along_axis(old_ref[:, span], to_lane, axis=1)
         weight = prior + counts
         cent = (prior * old + sums) / weight
-        cent_ref[:, span] = jnp.take_along_axis(cent, to_list, axis=1)
+        res_ref[CAP, :, span] = cent
         stat_ref[:, span] = jnp.concatenate([prior, weight, jnp.zeros((6, LANES), f32)], axis=0)
         for j in range(CAP):
             res = res_ref[j, :, span] - cent * seen[j]
@@ -171,13 +191,12 @@
     return pl.pallas_call(
         place_kernel,
         out_shape=(
-            jax.ShapeDtypeStruct((D, LISTS), f32),
-            jax.ShapeDtypeStruct((CAP, D, LISTS), f32),
+            jax.ShapeDtypeStruct((CAP + 1, D, LISTS), f32),
             jax.ShapeDtypeStruct((8, LISTS), f32),
             jax.ShapeDtypeStruct((DEV, LANES), f32),
         ),
         in_specs=[VMEM] * 3,
-        out_specs=(VMEM,) * 4,
+        out_specs=(VMEM,) * 3,
         scratch_shapes=[
             pltpu.VMEM((CELLS + 8, LANES), f32),
             pltpu.VMEM((DEV * (SEND - MAIN), LANES), f32),
@@ -185,11 +204,31 @@
             pltpu.SMEM((DEV, LANES), jnp.int32),
             pltpu.SemaphoreType.DMA,
         ],
+        compiler_params=pltpu.CompilerParams(vmem_limit_bytes=GRANT),
         name="place",
     )(got, old_centroids, prior_counts.reshape(1, LISTS))
 
 
-def gram_kernel(res_ref, gram_ref):
+def weave(parts, lane):
+    parts = list(parts)
+    for bit in (8, 4, 2, 1):
+        low = jnp.bitwise_and(lane, bit) == 0
+        for j in range(CAP):
+            if j & bit == 0:
+                one, two = parts[j], parts[j | bit]
+                parts[j] = jnp.where(low, one, pltpu.roll(two, bit, 1))
+                parts[j | bit] = jnp.where(low, pltpu.roll(one, LANES - bit, 1), two)
+    return parts
+
+
+def gram_kernel(res_ref, woven_ref, out_ref, gram_ref):
+    f32, i32 = jnp.float32, jnp.int32
+    lane = lax.broadcasted_iota(i32, (D, LANES), 1)
+    to_list = jnp.bitwise_and(lane, 7) * 16 + lax.shift_right_logical(lane, 3)
+    for h in range(LISTS // LANES):
+        span = slice(h * LANES, (h + 1) * LANES)
+        out_ref[:, span] = jnp.take_along_axis(res_ref[CAP, :, span], to_list, axis=1)
+
     def row(i, carry):
         for h in range(LISTS // LANES):
             span = slice(h * LANES, (h + 1) * LANES)
@@ -203,20 +242,42 @@
 
     lax.fori_loop(0, CAP, row, 0)
 
+    def spread(t, carry):
+        tile = pl.ds(pl.multiple_of(t * 8, 8), 8)
+        for h in range(LISTS // LANES):
+            span = slice(h * LANES, (h + 1) * LANES)
+            parts = weave([res_ref[j, tile, span] for j in range(CAP)], lane[:8])
+            for j in range(CAP):
+                at = (h * CAP + j) * LANES
+                woven_ref[tile, at : at + LANES] = parts[j]
+        return carry
+
+    lax.fori_loop(0, D // 8, spread, 0)
+    for h in range(LISTS // LANES):
+        for i in range(CAP):
+            at = (h * CAP + i) * LANES
+            woven_ref[D:, at : at + LANES] = gram_ref[h, i]
+
 
 def gram(res):
+    f32 = jnp.float32
     return pl.pallas_call(
         gram_kernel,
-        out_shape=jax.ShapeDtypeStruct((LISTS // LANES, CAP, CAP, LANES), jnp.float32),
+        out_shape=(
+            jax.ShapeDtypeStruct((D + CAP, CELLS), f32),
+            jax.ShapeDtypeStruct((D, LISTS), f32),
+        ),
         in_specs=[VMEM],
-        out_specs=VMEM,
-        cost_estimate=pl.CostEstimate(flops=2 * CAP * CAP * D * LISTS, bytes_accessed=4 * CAP * D * LISTS, transcendentals=0),
+        out_specs=(VMEM,) * 2,
+        scratch_shapes=[pltpu.VMEM((LISTS // LANES, CAP, CAP, LANES), f32)],
+        cost_estimate=pl.CostEstimate(flops=2 * CAP * CAP * D * LISTS, bytes_accessed=8 * CAP * D * LISTS, transcendentals=0),
+        compiler_params=pltpu.CompilerParams(vmem_limit_bytes=GRANT),
         name="gram",
     )(res)
 
 
-def whiten_kernel(res_ref, gram_ref, stat_ref, energy_ref, out_ref, t_ref, z_ref, s_ref, q_ref, o_ref):
-    f32, i32 = jnp.float32, jnp.int32
+def whiten_kernel(woven_ref, stat_ref, energy_ref, out_hbm, t_ref, z_ref, s_ref, q_ref, w_ref, out_ref, sem):
+    f32, bf16, i32 = jnp.float32, jnp.bfloat16, jnp.int32
     group = 4
     row_of = lax.broadcasted_iota(i32, (CAP, LANES), 0)
     energy = jnp.sum(energy_ref[...], axis=(0, 1), keepdims=True)
@@ -228,7 +289,8 @@
         ridge = shrinkage * stat_ref[0:1, span]
         frob = jnp.zeros((CAP, LANES), f32)
         for i in range(CAP):
-            row = (gram_ref[h, i] + jnp.where(row_of == i, ridge, 0.0)) * share
+            at = (h * CAP + i) * LANES
+            row = (woven_ref[D:, at : at + LANES] + jnp.where(row_of == i, ridge, 0.0)) * share
             t_ref[i] = row
             frob = frob + row * row
         ridge = ridge * share
@@ -271,65 +333,69 @@
             if step < STEPS - 1:
                 middle = [jnp.where(row_of == i, 1.5, 0.0) - 0.5 * t_ref[i] for i in range(CAP)]
 
-    lane = lax.broadcasted_iota(i32, (8, LANES), 1)
-    tiles = D // 8
-
-    def weave(n):
-        parts = [o_ref[j] for j in range(CAP)]
-
-        def finish():
-            h, t = n // tiles, n % tiles
-            for bit in (8, 4, 2, 1):
-                low = jnp.bitwise_and(lane, bit) == 0
-                for j in range(CAP):
-                    if j & bit == 0:
-                        one, two = parts[j], parts[j | bit]
-                        parts[j] = jnp.where(low, one, pltpu.roll(two, bit, 1))
-                        parts[j | bit] = jnp.where(low, pltpu.roll(one, LANES - bit, 1), two)
-            for j in range(CAP):
-                at = pl.multiple_of(h * (CAP * LANES) + j * LANES, LANES)
-                out_ref[pl.ds(pl.multiple_of(t * 8, 8), 8), pl.ds(at, LANES)] = parts[j]
-
-        return finish
-
-    def apply(n, carry):
-        finish = weave(jnp.maximum(n - 1, 0))
-        h, t = n // tiles, n % tiles
-        tile = pl.ds(pl.multiple_of(t * 8, 8), 8)
-        span = pl.ds(pl.multiple_of(h * LANES, LANES), LANES)
-        pieces = [res_ref[i, tile, span] for i in range(CAP)]
-        for j in range(CAP):
-            total = pieces[0] * q_ref[h, j, 0:1, :]
-            for i in range(1, CAP):
-                total = total + pieces[i] * q_ref[h, j, i : i + 1, :]
-            o_ref[j] = total
-        finish()
-        return carry
-
-    last = tiles * (LISTS // LANES)
-    lax.fori_loop(0, last, apply, 0)
-    weave(last - 1)()
-
-
-def whiten(res, gram_blocks, stat, energy):
+    lane = lax.broadcasted_iota(i32, (CAP, LANES), 1)
+    for h in range(LISTS // LANES):
+        for j, part in enumerate(weave([q_ref[h, i] for i in range(CAP)], lane)):
+            w_ref[h * CAP + j] = part
+    wide = 2 * LANES
+    block = lax.broadcasted_iota(i32, (LANES, LANES), 0) // CAP == lax.broadcasted_iota(i32, (LANES, LANES), 1) // CAP
+    empty = jnp.zeros((LANES, LANES), bf16)
+
+    def diagonal(first, second):
+        first, second = (
+            jnp.where(block, jnp.concatenate([x] * (LANES // CAP), axis=0), 0.0).astype(bf16) for x in (first, second)
+        )
+        return jnp.concatenate(
+            [jnp.concatenate([first, empty], axis=1), jnp.concatenate([empty, second], axis=1)], axis=0
+        )
+
+    copies = []
+    for g in range(CELLS // wide):
+        span = slice(g * wide, (g + 1) * wide)
+        pair = [w_ref[2 * g], w_ref[2 * g + 1]]
+        coarse = [x.astype(bf16).astype(f32) for x in pair]
+        fine = [x - y for x, y in zip(pair, coarse)]
+        coarse, fine = diagonal(*coarse), diagonal(*fine)
+        value = woven_ref[:D, span]
+        high = value.astype(bf16)
+        low = (value - high.astype(f32)).astype(bf16)
+        out_ref[:, span] = (
+            jnp.dot(high, coarse, preferred_element_type=f32)
+            + jnp.dot(low, coarse, preferred_element_type=f32)
+            + jnp.dot(high, fine, preferred_element_type=f32)
+        )
+        copies.append(pltpu.make_async_copy(out_ref.at[:, span], out_hbm.at[:, span], sem.at[g]))
+        copies[g].start()
+    for copy in copies:
+        copy.wait()
+
+
+def whiten(woven, stat, energy):
     f32 = jnp.float32
     return pl.pallas_call(
         whiten_kernel,
         out_shape=jax.ShapeDtypeStruct((D, CELLS), f32),
-        in_specs=[VMEM] * 4,
-        out_specs=VMEM,
+        in_specs=[VMEM] * 3,
+        out_specs=pl.BlockSpec(memory_space=pltpu.HBM),
         scratch_shapes=[pltpu.VMEM((CAP, CAP, LANES), f32)] * 3
-        + [pltpu.VMEM((LISTS // LANES, CAP, CAP, LANES), f32), pltpu.VMEM((CAP, 8, LANES), f32)],
+        + [
+            pltpu.VMEM((LISTS // LANES, CAP, CAP, LANES), f32),
+            pltpu.VMEM((CELLS // LANES, CAP, LANES), f32),
+            pltpu.VMEM((D, CELLS), f32),
+            pltpu.SemaphoreType.DMA((CELLS // (2 * LANES),)),
+        ],
+        compiler_params=pltpu.CompilerParams(vmem_limit_bytes=GRANT),
         name="whiten",
-    )(res, gram_blocks, stat, energy)
+    )(woven, stat, energy)
 
 
 def local(vectors, assignment, slot, old_centroids, prior_counts):
     outgoing = dispatch(vectors, assignment, slot).reshape(DEV, 1, BLOCK * LANES)
     incoming = lax.all_to_all(outgoing, AXES, split_axis=0, concat_axis=0, tiled=True)
-    centroids, res, stat, energy = place(incoming.reshape(DEV * BLOCK, LANES), old_centroids, prior_counts)
+    res, stat, energy = place(incoming.reshape(DEV * BLOCK, LANES), old_centroids, prior_counts)
     shared = lax.all_to_all(energy.reshape(DEV, 1, LANES), AXES, split_axis=0, concat_axis=0, tiled=True)
-    rotated = whiten(res, gram(res), stat, shared.reshape(DEV, LANES))
+    woven, centroids = gram(res)
+    rotated = whiten(woven, stat, shared.reshape(DEV, LANES))
     return (centroids, rotated)
 
 

time: 79.4 us -> 69.6 us (0.88)
  Pallas kernels: 30.2 us -> 22.7 us
  waiting for transfers between devices: 5.87 us -> 3.52 us
  starting transfers between devices: 4.63 us -> 5.59 us
    pallas_call x1, Pallas kernels: 12.9 us -> 6.51 us  [whiten(): pl.pallas_call(whiten_kernel, out_shape=jax.ShapeDtypeStruct((D, CELLS),...]
    all_to_all x1, waiting for transfers between devices: 5.87 us -> 3.52 us  [local(): lax.all_to_all(energy.reshape(DEV, 1, LANES), AXES, split_axis=0, concat_...]
    pallas_call x1, Pallas kernels: 6.35 us -> 4.76 us  [dispatch(): pl.pallas_call(dispatch_kernel, out_shape=jax.ShapeDtypeStruct((DEV * BLO...]
    all_to_all x1, starting transfers between devices: 4.63 us -> 5.59 us  [local(): lax.all_to_all(energy.reshape(DEV, 1, LANES), AXES, split_axis=0, concat_...]
  transfers between devices with their start and end apart: 1 -> 1, of which waited for: 1 -> 1; matrix products, arithmetic and copies ran while one was open for 0% -> 0% of each run, Pallas kernels for 5% -> 9%
where the time goes in v2:
time: 69.6 us; the launch traced here: 69.3 us
  blocking collectives  36.8 us (53%)
  Pallas kernels  22.7 us (33%)
  starting transfers between devices  5.59 us (8%)
  waiting for transfers between devices  3.52 us (5%)
    all_to_all x1, blocking collectives, local(): lax.all_to_all(outgoing, AXES, split_axis=0, concat_axis=0, tiled=True)  36.8 us
    pallas_call x1, Pallas kernels, whiten(): pl.pallas_call(whiten_kernel, out_shape=jax.ShapeDtypeStruct((D, CELLS),...  6.51 us
    pallas_call x1, Pallas kernels, gram(): pl.pallas_call(gram_kernel, out_shape=(jax.ShapeDtypeStruct((D + CAP, CEL...  5.95 us
    all_to_all x1, starting transfers between devices, local(): lax.all_to_all(energy.reshape(DEV, 1, LANES), AXES, split_axis=0, concat_...  5.59 us
    pallas_call x1, Pallas kernels, place(): pl.pallas_call(place_kernel, out_shape=(jax.ShapeDtypeStruct((CAP + 1, D,...  5.49 us
    pallas_call x1, Pallas kernels, dispatch(): pl.pallas_call(dispatch_kernel, out_shape=jax.ShapeDtypeStruct((DEV * BLO...  4.76 us
    all_to_all x1, waiting for transfers between devices, local(): lax.all_to_all(energy.reshape(DEV, 1, LANES), AXES, split_axis=0, concat_...  3.52 us
  transfers between devices with their start and end apart: 1, of which 1 were waited for; matrix products, arithmetic and copies ran while one was open for 0% of the time, Pallas kernels for 9%

profile of v2, /device:TPU:1, one launch (start us, length us, event | category | flops | bytes accessed | tf_op | source)
XLA Modules:
  0.0 69.3 jit_solution(15306306992197639675)
XLA Ops:
  0.6 4.8 %dispatch.1 = f32[3200,128]{1,0:T(8,128)S(1)} custom-call(f32[96,2048]{1,0:T(8,128)} %vec_hbm.1, s32[16,128]{1,0:T(8,128)} %bitcast.12, s32[16,128]{1,0:T(8,128)} %bitcast.13), custom_call_target="tpu_custom_call" | custom-call | tf_op jit(solution)/shard_map/dispatch/pallas_call | solution.py:107
  5.4 0.0 copy-start
  5.4 0.0 copy-start.1
  5.4 36.8 %all_to_all.10 = f32[128,1,3200]{2,1,0:T(1,128)S(1)} all-to-all(f32[128,1,3200]{2,1,0:T(1,128)S(1)} %bitcast.10), channel_id=1, replica_groups=mesh['dp'=16,'owner'=8] {'dp','owner'}, dimensions={0} | all-to-all | bytes 3276800 | tf_op jit(solution)/shard_map/all_to_all | solution.py:394
  42.2 0.0 copy-done
  42.2 0.0 copy-done.1
  42.2 5.5 %place.1 = (f32[17,96,256]{2,1,0:T(8,128)S(1)}, f32[8,256]{1,0:T(8,128)S(1)}, f32[128,128]{1,0:T(8,128)}) custom-call(f32[3200,128]{1,0:T(8,128)S(1)} %bitcast.9, f32[96,256]{1,0:T(8,128)S(1)} %copy-done, s32[1,256]{1,0:T(1,128)S(1)} %bitcast.11), custom_call_target="tpu_custom_call" | custom-call | tf_op jit(solution)/shard_map/place/pallas_call | solution.py:191
  47.7 5.6 %all-to-all-start.1 = ((f32[128,1,128]{2,1,0:T(1,128)}), f32[128,1,128]{2,1,0:T(1,128)}, u32[]{:S(2)}, u32[]{:S(2)}) async-start(f32[128,1,128]{2,1,0:T(1,128)} %bitcast.6), calls=%async_computation.1 | async-start | bytes 131072 | tf_op jit(solution)/shard_map/all_to_all | solution.py:396
  53.3 6.0 %gram.1 = (f32[112,4096]{1,0:T(8,128)S(1)}, f32[96,256]{1,0:T(8,128)}) custom-call(f32[17,96,256]{2,1,0:T(8,128)S(1)} %get-tuple-element.7.res_ref), custom_call_target="tpu_custom_call" | custom-call | flops 12582912 | bytes 3145728 | tf_op jit(solution)/shard_map/gram/pallas_call | solution.py:264
  59.3 3.5 %all-to-all-done.1 = f32[128,1,128]{2,1,0:T(1,128)} async-done(((f32[128,1,128]{2,1,0:T(1,128)}), f32[128,1,128]{2,1,0:T(1,128)}, u32[]{:S(2)}, u32[]{:S(2)}) %all-to-all-start.1) | async-done | bytes 65568 | tf_op jit(solution)/shard_map/all_to_all | solution.py:396
  62.8 6.5 %whiten.1 = f32[96,4096]{1,0:T(8,128)} custom-call(f32[112,4096]{1,0:T(8,128)S(1)} %get-tuple-element.9.woven_ref, f32[8,256]{1,0:T(8,128)S(1)} %get-tuple-element.10.stat_ref, f32[128,128]{1,0:T(8,128)} %bitcast.7.energy_ref), custom_call_target="tpu_custom_call" | custom-call | tf_op jit(solution)/shard_map/whiten/pallas_call | solution.py:375
Async XLA Ops:
  5.4 36.8 %copy-start = (f32[96,256]{1,0:T(8,128)S(1)}, f32[96,256]{1,0:T(8,128)}, u32[]{:S(2)}) copy-start(f32[96,256]{1,0:T(8,128)} %old_ref.1) | copy-start | bytes 294916
  5.4 36.8 %copy-start.1 = (s32[256]{0:T(256)S(1)}, s32[256]{0:T(256)}, u32[]{:S(2)}) copy-start(s32[256]{0:T(256)} %param.9) | copy-start | bytes 3076
  47.7 15.1 %all-to-all-start.1 = ((f32[128,1,128]{2,1,0:T(1,128)}), f32[128,1,128]{2,1,0:T(1,128)}, u32[]{:S(2)}, u32[]{:S(2)}) async-start(f32[128,1,128]{2,1,0:T(1,128)} %bitcast.6), calls=%async_computation.1 | async-start | bytes 131072 | tf_op jit(solution)/shard_map/all_to_all | solution.py:396

commit v3 on v2

--- a/solution.py
+++ b/solution.py
@@ -18,12 +18,14 @@
 TAIL = D - CAP
 MAIN = 24
 BLOCK = MAIN + 1
+POWERS = 4
 TOTAL = D * TOK * DEV
 
 shrink_weight = 0.5
 epsilon = 1e-05
 
 VMEM = pl.BlockSpec(memory_space=pltpu.VMEM)
+HBM = pl.BlockSpec(memory_space=pltpu.HBM)
 GRANT = 16 * 1024 * 1024
 
 
@@ -124,7 +126,7 @@
     )(*(pltpu.with_memory_space_constraint(x, pltpu.HBM) for x in arrays))
 
 
-def place_kernel(got_ref, old_ref, prior_ref, res_ref, stat_ref, energy_ref, cells, tails, lab_v, lab_s, sem):
+def place_kernel(got_ref, old_ref, prior_ref, res_hbm, stat_ref, energy_ref, res_ref, cells, tails, lab_v, lab_s, sem, out_sem):
     f32, i32 = jnp.float32, jnp.int32
     lab_v[...] = got_ref[pl.ds(MAIN, DEV, stride=BLOCK), :].astype(i32)
     copy = pltpu.make_async_copy(lab_v, lab_s, sem)
@@ -137,24 +139,24 @@
             pltpu.roll(got_ref[pl.ds(d * BLOCK + 8 * k, 8), :], 32 * k + 32, 1) for k in range(MAIN // 8)
         )
         tail = jnp.where(near < 32, first, jnp.where(near < 64, second, third))
-        tails[pl.ds(pl.multiple_of(8 * d, 8), 8), :] = tail
+        tails[pl.ds(pl.multiple_of(d * (SEND - MAIN), 8), 8), :] = tail
         return carry
 
     lax.fori_loop(0, DEV, unpack, 0, unroll=8)
     copy.wait()
 
     def move(d, carry):
-        labels = lab_s.at[d]
         for r in range(MAIN):
-            cells[pl.ds(labels[r], 1), :] = got_ref[pl.ds(d * BLOCK + r, 1), :]
+            cells[pl.ds(lab_s[d, r], 1), :] = got_ref[pl.ds(d * BLOCK + r, 1), :]
         for r in range(MAIN, SEND):
-            cells[pl.ds(labels[r], 1), :] = tails[pl.ds(d * (SEND - MAIN) + r - MAIN, 1), :]
+            cells[pl.ds(lab_s[d, r], 1), :] = tails[pl.ds(d * (SEND - MAIN) + r - MAIN, 1), :]
         return carry
 
     lax.fori_loop(0, DEV, move, 0, unroll=True)
     lane = lax.broadcasted_iota(i32, (D, LANES), 1)
     to_lane = jnp.bitwise_and(lane, 15) * 8 + lax.shift_right_logical(lane, 4)
     total = jnp.zeros((8, LANES), f32)
+    outs = []
     for h in range(LISTS // LANES):
         span = slice(h * LANES, (h + 1) * LANES)
         sums = jnp.zeros((D, LANES), f32)
@@ -183,7 +185,11 @@
             square = res * res
             for t in range(D // 8):
                 total = total + square[8 * t : 8 * t + 8]
+        outs.append(pltpu.make_async_copy(res_ref.at[:, :, span], res_hbm.at[:, :, span], out_sem.at[h]))
+        outs[h].start()
     energy_ref[...] = jnp.broadcast_to(jnp.sum(total, axis=0, keepdims=True), (DEV, LANES))
+    for out in outs:
+        out.wait()
 
 
 def place(got, old_centroids, prior_counts):
@@ -191,18 +197,20 @@
     return pl.pallas_call(
         place_kernel,
         out_shape=(
-            jax.ShapeDtypeStruct((CAP + 1, D, LISTS), f32),
+            pltpu.HBM((CAP + 1, D, LISTS), f32),
             jax.ShapeDtypeStruct((8, LISTS), f32),
             jax.ShapeDtypeStruct((DEV, LANES), f32),
         ),
         in_specs=[VMEM] * 3,
-        out_specs=(VMEM,) * 3,
+        out_specs=(HBM, VMEM, VMEM),
         scratch_shapes=[
+            pltpu.VMEM((CAP + 1, D, LISTS), f32),
             pltpu.VMEM((CELLS + 8, LANES), f32),
             pltpu.VMEM((DEV * (SEND - MAIN), LANES), f32),
             pltpu.VMEM((DEV, LANES), jnp.int32),
             pltpu.SMEM((DEV, LANES), jnp.int32),
             pltpu.SemaphoreType.DMA,
+            pltpu.SemaphoreType.DMA((LISTS // LANES,)),
         ],
         compiler_params=pltpu.CompilerParams(vmem_limit_bytes=GRANT),
         name="place",
@@ -221,8 +229,18 @@
     return parts
 
 
-def gram_kernel(res_ref, woven_ref, out_ref, gram_ref):
+def times(left, i, right):
+    total = left[i, 0:1, :] * right[0]
+    for k in range(1, CAP):
+        total = total + left[i, k : k + 1, :] * right[k]
+    return total
+
+
+def gram_kernel(res_hbm, woven_ref, out_ref, gram_ref, next_ref, res_ref, sem):
     f32, i32 = jnp.float32, jnp.int32
+    get = pltpu.make_async_copy(res_hbm, res_ref, sem)
+    get.start()
+    get.wait()
     lane = lax.broadcasted_iota(i32, (D, LANES), 1)
     to_list = jnp.bitwise_and(lane, 7) * 16 + lax.shift_right_logical(lane, 3)
     for h in range(LISTS // LANES):
@@ -253,10 +271,34 @@
         return carry
 
     lax.fori_loop(0, D // 8, spread, 0)
+    group = 4
     for h in range(LISTS // LANES):
+        trace = gram_ref[h, 0, 0:1, :]
+        for i in range(1, CAP):
+            trace = trace + gram_ref[h, i, i : i + 1, :]
+        trace = jnp.where(trace > 0.0, trace, 1.0)
+        woven_ref[D + POWERS * CAP :, h * LANES : (h + 1) * LANES] = jnp.broadcast_to(trace, (8, LANES))
+        unit = 1.0 / trace
+        base = []
         for i in range(CAP):
+            row = gram_ref[h, i] * unit
+            base.append(row)
+            next_ref[0, i] = row
             at = (h * CAP + i) * LANES
-            woven_ref[D:, at : at + LANES] = gram_ref[h, i]
+            woven_ref[D : D + CAP, at : at + LANES] = row
+
+        def raise_rows(block, carry, h=h, base=base):
+            spots = [block * group + g for g in range(group)]
+            for power in range(1, POWERS):
+                for i in spots:
+                    row = times(next_ref.at[power - 1], i, base)
+                    if power < POWERS - 1:
+                        next_ref[power, i] = row
+                    at = pl.multiple_of((h * CAP + i) * LANES, LANES)
+                    woven_ref[D + power * CAP : D + (power + 1) * CAP, pl.ds(at, LANES)] = row
+            return carry
+
+        lax.fori_loop(0, CAP // group, raise_rows, 0)
 
 
 def gram(res):
@@ -264,16 +306,21 @@
     return pl.pallas_call(
         gram_kernel,
         out_shape=(
-            jax.ShapeDtypeStruct((D + CAP, CELLS), f32),
+            jax.ShapeDtypeStruct((D + POWERS * CAP + 8, CELLS), f32),
             jax.ShapeDtypeStruct((D, LISTS), f32),
         ),
-        in_specs=[VMEM],
+        in_specs=[HBM],
         out_specs=(VMEM,) * 2,
-        scratch_shapes=[pltpu.VMEM((LISTS // LANES, CAP, CAP, LANES), f32)],
+        scratch_shapes=[
+            pltpu.VMEM((LISTS // LANES, CAP, CAP, LANES), f32),
+            pltpu.VMEM((POWERS - 1, CAP, CAP, LANES), f32),
+            pltpu.VMEM((CAP + 1, D, LISTS), f32),
+            pltpu.SemaphoreType.DMA,
+        ],
         cost_estimate=pl.CostEstimate(flops=2 * CAP * CAP * D * LISTS, bytes_accessed=8 * CAP * D * LISTS, transcendentals=0),
         compiler_params=pltpu.CompilerParams(vmem_limit_bytes=GRANT),
         name="gram",
-    )(res)
+    )(pltpu.with_memory_space_constraint(res, pltpu.HBM))
 
 
 def whiten_kernel(woven_ref, stat_ref, energy_ref, out_hbm, t_ref, z_ref, s_ref, q_ref, w_ref, out_ref, sem):
@@ -284,39 +331,50 @@
     shrinkage = shrink_weight * energy / TOTAL + epsilon
     for h in range(LISTS // LANES):
         span = slice(h * LANES, (h + 1) * LANES)
-        weight = stat_ref[1:2, span]
+        prior, weight = stat_ref[0:1, span], stat_ref[1:2, span]
+        trace = woven_ref[D + POWERS * CAP : D + POWERS * CAP + 1, span]
         share = 1.0 / weight
-        ridge = shrinkage * stat_ref[0:1, span]
+        ridge = shrinkage * prior * share
+        trace = trace * share
+
+        def power(k, i):
+            at = (h * CAP + i) * LANES
+            return woven_ref[D + k * CAP : D + (k + 1) * CAP, at : at + LANES]
+
         frob = jnp.zeros((CAP, LANES), f32)
         for i in range(CAP):
-            at = (h * CAP + i) * LANES
-            row = (woven_ref[D:, at : at + LANES] + jnp.where(row_of == i, ridge, 0.0)) * share
-            t_ref[i] = row
+            row = trace * power(0, i) + jnp.where(row_of == i, ridge, 0.0)
             frob = frob + row * row
-        ridge = ridge * share
         frob = jnp.sqrt(jnp.sum(frob, axis=0, keepdims=True) + TAIL * (ridge * ridge))
         scale = 1.0 / frob
+        a, x = trace * scale, ridge * scale
+        t0 = x * (2.25 + x * (0.25 * x - 1.5))
+        t1 = a * (2.25 + x * (0.75 * x - 3.0))
+        t2 = a * a * (0.75 * x - 1.5)
+        t3 = a * a * a * 0.25
+        z0 = 2.25 + x * (-2.4375 + x * (1.6875 + x * (0.0625 * x - 0.5625)))
+        z1 = a * (-2.4375 + x * (3.375 + x * (0.25 * x - 1.6875)))
+        z2 = a * a * (1.6875 + x * (0.375 * x - 1.6875))
+        z3 = a * a * a * (0.25 * x - 0.5625)
+        z4 = a * a * (a * a) * 0.0625
         middle = []
         for i in range(CAP):
-            row = t_ref[i] * scale
+            own = row_of == i
+            h1, h2, h3, h4 = (power(k, i) for k in range(POWERS))
+            row = t1 * h1 + t2 * h2 + t3 * h3 + jnp.where(own, t0, 0.0)
             t_ref[i] = row
-            middle.append(jnp.where(row_of == i, 1.5, 0.0) - 0.5 * row)
-            z_ref[i] = middle[i]
-
-        def times(left, i, middle):
-            total = left[i, 0:1, :] * middle[0]
-            for k in range(1, CAP):
-                total = total + left[i, k : k + 1, :] * middle[k]
-            return total
-
-        for step in range(STEPS):
-
-            def advance(block, carry, step=step, middle=middle):
+            z_ref[i] = z1 * h1 + z2 * h2 + z3 * h3 + z4 * h4 + jnp.where(own, z0, 0.0)
+            middle.append(jnp.where(own, 1.5, 0.0) - 0.5 * row)
+        root = 1.0 / jnp.sqrt(frob)
+
+        for step in range(1, STEPS):
+
+            def advance(block, carry, step=step, middle=middle, root=root, h=h):
                 spots = [block * group + g for g in range(group)]
                 if step < STEPS - 1:
                     for i in spots:
                         s_ref[i] = times(t_ref, i, middle)
-                if step > 0:
+                if step > 1:
                     for i in spots:
                         moved = times(z_ref, i, middle)
                         if step == STEPS - 1:
@@ -328,7 +386,6 @@
                         t_ref[i] = times(s_ref, i, middle)
                 return carry
 
-            root = 1.0 / jnp.sqrt(frob)
             lax.fori_loop(0, CAP // group, advance, 0)
             if step < STEPS - 1:
                 middle = [jnp.where(row_of == i, 1.5, 0.0) - 0.5 * t_ref[i] for i in range(CAP)]

time: 69.6 us -> 67.7 us (0.973)
  waiting for transfers between devices: 3.52 us -> 0.96 us
  Pallas kernels: 22.7 us -> 24.4 us
  starting transfers between devices: 5.59 us -> 4.63 us
    pallas_call x2, Pallas kernels: 11.4 us -> 14.7 us  [the longest x1 8.48 us: gram(): pl.pallas_call(gram_kernel, out_shape=(jax.ShapeDtypeStruct((D + POWERS *...]
    all_to_all x1, waiting for transfers between devices: 3.52 us -> 0.96 us  [local(): lax.all_to_all(energy.reshape(DEV, 1, LANES), AXES, split_axis=0, concat_...]
    pallas_call x1, Pallas kernels: 6.51 us -> 4.91 us  [whiten(): pl.pallas_call(whiten_kernel, out_shape=jax.ShapeDtypeStruct((D, CELLS),...]
    all_to_all x1, starting transfers between devices: 5.59 us -> 4.63 us  [local(): lax.all_to_all(energy.reshape(DEV, 1, LANES), AXES, split_axis=0, concat_...]
  transfers between devices with their start and end apart: 1 -> 1, of which waited for: 1 -> 1; matrix products, arithmetic and copies ran while one was open for 0% -> 0% of each run, Pallas kernels for 9% -> 13%
where the time goes in v3:
time: 67.7 us; the launch traced here: 67.5 us
  blocking collectives  36.8 us (54%)
  Pallas kernels  24.4 us (36%)
  starting transfers between devices  4.63 us (7%)
  waiting for transfers between devices  0.96 us (1%)
  between operations  0.68 us (1%)
    all_to_all x1, blocking collectives, local(): lax.all_to_all(outgoing, AXES, split_axis=0, concat_axis=0, tiled=True)  36.8 us
    pallas_call x1, Pallas kernels, gram(): pl.pallas_call(gram_kernel, out_shape=(jax.ShapeDtypeStruct((D + POWERS *...  8.48 us
    pallas_call x1, Pallas kernels, place(): pl.pallas_call(place_kernel, out_shape=(pltpu.HBM((CAP + 1, D, LISTS), f3...  6.26 us
    pallas_call x1, Pallas kernels, whiten(): pl.pallas_call(whiten_kernel, out_shape=jax.ShapeDtypeStruct((D, CELLS),...  4.91 us
    pallas_call x1, Pallas kernels, dispatch(): pl.pallas_call(dispatch_kernel, out_shape=jax.ShapeDtypeStruct((DEV * BLO...  4.76 us
    all_to_all x1, starting transfers between devices, local(): lax.all_to_all(energy.reshape(DEV, 1, LANES), AXES, split_axis=0, concat_...  4.63 us
  transfers between devices with their start and end apart: 1, of which 1 were waited for; matrix products, arithmetic and copies ran while one was open for 0% of the time, Pallas kernels for 13%

profile of v3, /device:TPU:1, one launch (start us, length us, event | category | flops | bytes accessed | tf_op | source)
XLA Modules:
  0.0 67.5 jit_solution(8494003468692592512)
XLA Ops:
  0.6 4.8 %dispatch.1 = f32[3200,128]{1,0:T(8,128)S(1)} custom-call(f32[96,2048]{1,0:T(8,128)} %vec_hbm.1, s32[16,128]{1,0:T(8,128)} %bitcast.13, s32[16,128]{1,0:T(8,128)} %bitcast.14), custom_call_target="tpu_custom_call" | custom-call | tf_op jit(solution)/shard_map/dispatch/pallas_call | solution.py:109
  5.4 0.0 copy-start
  5.4 0.0 copy-start.1
  5.4 36.8 %all_to_all.10 = f32[128,1,3200]{2,1,0:T(1,128)S(1)} all-to-all(f32[128,1,3200]{2,1,0:T(1,128)S(1)} %bitcast.10), channel_id=1, replica_groups=mesh['dp'=16,'owner'=8] {'dp','owner'}, dimensions={0} | all-to-all | bytes 3276800 | tf_op jit(solution)/shard_map/all_to_all | solution.py:451
  42.2 0.0 copy-done
  42.2 0.0 copy-done.1
  42.2 6.3 %place.1 = (f32[17,96,256]{2,1,0:T(8,128)}, f32[8,256]{1,0:T(8,128)S(1)}, f32[128,128]{1,0:T(8,128)}) custom-call(f32[3200,128]{1,0:T(8,128)S(1)} %bitcast.9, f32[96,256]{1,0:T(8,128)S(1)} %copy-done, s32[1,256]{1,0:T(1,128)S(1)} %bitcast.12), custom_call_target="tpu_custom_call" | custom-call | tf_op jit(solution)/shard_map/place/pallas_call | solution.py:197
  48.5 4.6 %all-to-all-start.1 = ((f32[128,1,128]{2,1,0:T(1,128)}), f32[128,1,128]{2,1,0:T(1,128)S(1)}, u32[]{:S(2)}, u32[]{:S(2)}) async-start(f32[128,1,128]{2,1,0:T(1,128)} %bitcast.6), calls=%async_computation.1 | async-start | bytes 131072 | tf_op jit(solution)/shard_map/all_to_all | solution.py:453
  53.1 8.5 %gram.1 = (f32[168,4096]{1,0:T(8,128)S(1)}, f32[96,256]{1,0:T(8,128)}) custom-call(f32[17,96,256]{2,1,0:T(8,128)} %get-tuple-element.7.res_hbm), custom_call_target="tpu_custom_call" | custom-call | flops 12582912 | bytes 3145728 | tf_op jit(solution)/shard_map/gram/pallas_call | solution.py:306
  61.6 1.0 %all-to-all-done.1 = f32[128,1,128]{2,1,0:T(1,128)S(1)} async-done(((f32[128,1,128]{2,1,0:T(1,128)}), f32[128,1,128]{2,1,0:T(1,128)S(1)}, u32[]{:S(2)}, u32[]{:S(2)}) %all-to-all-start.1) | async-done | bytes 65568 | tf_op jit(solution)/shard_map/all_to_all | solution.py:453
  62.6 4.9 %whiten.1 = f32[96,4096]{1,0:T(8,128)} custom-call(f32[168,4096]{1,0:T(8,128)S(1)} %get-tuple-element.9.woven_ref, f32[8,256]{1,0:T(8,128)S(1)} %get-tuple-element.10.stat_ref, f32[128,128]{1,0:T(8,128)S(1)} %bitcast.11), custom_call_target="tpu_custom_call" | custom-call | tf_op jit(solution)/shard_map/whiten/pallas_call | solution.py:432
Async XLA Ops:
  5.4 36.8 %copy-start = (f32[96,256]{1,0:T(8,128)S(1)}, f32[96,256]{1,0:T(8,128)}, u32[]{:S(2)}) copy-start(f32[96,256]{1,0:T(8,128)} %old_ref.1) | copy-start | bytes 294916
  5.4 36.8 %copy-start.1 = (s32[256]{0:T(256)S(1)}, s32[256]{0:T(256)}, u32[]{:S(2)}) copy-start(s32[256]{0:T(256)} %param.9) | copy-start | bytes 3076
  48.5 14.1 %all-to-all-start.1 = ((f32[128,1,128]{2,1,0:T(1,128)}), f32[128,1,128]{2,1,0:T(1,128)S(1)}, u32[]{:S(2)}, u32[]{:S(2)}) async-start(f32[128,1,128]{2,1,0:T(1,128)} %bitcast.6), calls=%async_computation.1 | async-start | bytes 131072 | tf_op jit(solution)/shard_map/all_to_all | solution.py:453

commit v4 on v3

--- a/solution.py
+++ b/solution.py
@@ -57,13 +57,15 @@
     row2 = lax.broadcasted_iota(i32, (wide, wide), 0)
     col2 = lax.broadcasted_iota(i32, (wide, wide), 1)
     before = jnp.concatenate([jnp.where(row2 < col2, 1.0, 0.0), jnp.ones((wide, wide), f32)], axis=1).astype(bf16)
+    picks = [sub == pair(owner, c) for c in range(TOK // wide)]
+    hots = [jnp.where(x, 1.0, 0.0).astype(bf16) for x in picks]
+    counts = jnp.dot(jnp.concatenate(hots, axis=0), before, preferred_element_type=f32)
     carry = jnp.zeros((LANES, wide), f32)
     codes = jnp.zeros((LANES, 2 * SEND), f32)
     for c in range(TOK // wide):
         mine = pair(owner, c)
-        picked = sub == mine
-        hot = jnp.where(picked, 1.0, 0.0).astype(bf16)
-        counted = jnp.dot(hot, before, preferred_element_type=f32)
+        picked, hot = picks[c], hots[c]
+        counted = counts[c * LANES : (c + 1) * LANES]
         rank = jnp.sum(jnp.where(picked, counted[:, :wide] + carry, 0.0), axis=0, keepdims=True).astype(i32)
         carry = carry + counted[:, wide:]
         pos = jnp.where(rank < MAIN, mine * BLOCK + rank, DEV * BLOCK - MAIN + mine * (SEND - MAIN) + rank)
@@ -80,10 +82,10 @@
     labels = jnp.where(labels < 0.0, float(CELLS), labels)
     labels = jnp.concatenate([labels, jnp.zeros((DEV, LANES - SEND), f32)], axis=1)
     send_ref[pl.ds(MAIN, DEV, stride=BLOCK), :] = labels
-    fill = jnp.zeros((LANES - D, LANES), f32)
     get_vectors.wait()
     for c in range(TOK // LANES):
-        block = jnp.concatenate([vec_ref[:, c * LANES : (c + 1) * LANES], fill], axis=0)
+        block = vec_ref[:, c * LANES : (c + 1) * LANES]
+        block = jnp.concatenate([block, block[: LANES - D]], axis=0)
         rows[c * LANES : (c + 1) * LANES, :] = block.T
     copy.wait()
 
@@ -98,7 +100,7 @@
         tail = stage[pl.ds(pl.multiple_of(DEV * BLOCK + 8 * d, 8), 8), :]
         for k in range(MAIN // 8):
             spot = pl.ds(d * BLOCK + 8 * k, 8)
-            send_ref[spot, :] = jnp.where(outer, pltpu.roll(tail, D - 32 * k, 1), stage[spot, :])
+            send_ref[spot, :] = jnp.where(outer, pltpu.roll(tail, D - 32 * k, 1) if k else tail, stage[spot, :])
         return carry
 
     lax.fori_loop(0, DEV, pack, 0, unroll=8)
@@ -157,6 +159,15 @@
     to_lane = jnp.bitwise_and(lane, 15) * 8 + lax.shift_right_logical(lane, 4)
     total = jnp.zeros((8, LANES), f32)
     outs = []
+    gathered = []
+    part = 4
+
+    def send(h, planes):
+        outs.append(
+            pltpu.make_async_copy(res_ref.at[h, planes], res_hbm.at[h, planes], out_sem.at[len(outs)])
+        )
+        outs[-1].start()
+
     for h in range(LISTS // LANES):
         span = slice(h * LANES, (h + 1) * LANES)
         sums = jnp.zeros((D, LANES), f32)
@@ -171,22 +182,27 @@
             sums = sums + block
             counts = counts + here
             seen.append(here)
-            res_ref[j, :, span] = block
+            res_ref[h, j] = block
+            if j % part == part - 1:
+                send(h, slice(j + 1 - part, j + 1))
         prior8 = jnp.broadcast_to(prior_ref[:, span].astype(f32), (8, LANES))
         prior = jnp.take_along_axis(prior8, to_lane[:8], axis=1)[:1]
         old = jnp.take_along_axis(old_ref[:, span], to_lane, axis=1)
         weight = prior + counts
         cent = (prior * old + sums) / weight
-        res_ref[CAP, :, span] = cent
+        res_ref[h, CAP] = cent
+        res_ref[h, CAP + 1, :CAP] = jnp.concatenate(seen, axis=0)
+        res_ref[h, CAP + 1, CAP:] = jnp.zeros((D - CAP, LANES), f32)
         stat_ref[:, span] = jnp.concatenate([prior, weight, jnp.zeros((6, LANES), f32)], axis=0)
+        send(h, slice(CAP, CAP + 2))
+        gathered.append((cent, seen))
+    for h, (cent, seen) in enumerate(gathered):
+        span = slice(h * LANES, (h + 1) * LANES)
         for j in range(CAP):
-            res = res_ref[j, :, span] - cent * seen[j]
-            res_ref[j, :, span] = res
+            res = res_ref[h, j] - cent * seen[j]
             square = res * res
             for t in range(D // 8):
                 total = total + square[8 * t : 8 * t + 8]
-        outs.append(pltpu.make_async_copy(res_ref.at[:, :, span], res_hbm.at[:, :, span], out_sem.at[h]))
-        outs[h].start()
     energy_ref[...] = jnp.broadcast_to(jnp.sum(total, axis=0, keepdims=True), (DEV, LANES))
     for out in outs:
         out.wait()
@@ -197,20 +213,20 @@
     return pl.pallas_call(
         place_kernel,
         out_shape=(
-            pltpu.HBM((CAP + 1, D, LISTS), f32),
+            pltpu.HBM((LISTS // LANES, CAP + 2, D, LANES), f32),
             jax.ShapeDtypeStruct((8, LISTS), f32),
             jax.ShapeDtypeStruct((DEV, LANES), f32),
         ),
         in_specs=[VMEM] * 3,
         out_specs=(HBM, VMEM, VMEM),
         scratch_shapes=[
-            pltpu.VMEM((CAP + 1, D, LISTS), f32),
+            pltpu.VMEM((LISTS // LANES, CAP + 2, D, LANES), f32),
             pltpu.VMEM((CELLS + 8, LANES), f32),
             pltpu.VMEM((DEV * (SEND - MAIN), LANES), f32),
             pltpu.VMEM((DEV, LANES), jnp.int32),
             pltpu.SMEM((DEV, LANES), jnp.int32),
             pltpu.SemaphoreType.DMA,
-            pltpu.SemaphoreType.DMA((LISTS // LANES,)),
+            pltpu.SemaphoreType.DMA((10,)),
         ],
         compiler_params=pltpu.CompilerParams(vmem_limit_bytes=GRANT),
         name="place",
@@ -245,15 +261,18 @@
     to_list = jnp.bitwise_and(lane, 7) * 16 + lax.shift_right_logical(lane, 3)
     for h in range(LISTS // LANES):
         span = slice(h * LANES, (h + 1) * LANES)
-        out_ref[:, span] = jnp.take_along_axis(res_ref[CAP, :, span], to_list, axis=1)
+        cent = res_ref[h, CAP]
+        out_ref[:, span] = jnp.take_along_axis(cent, to_list, axis=1)
+        for j in range(CAP):
+            res_ref[h, j] = res_ref[h, j] - cent * res_ref[h, CAP + 1, j : j + 1]
 
     def row(i, carry):
         for h in range(LISTS // LANES):
             span = slice(h * LANES, (h + 1) * LANES)
-            left = res_ref[i, :, span]
+            left = res_ref[h, i]
             for step in range(CAP // 2 + 1):
                 j = jnp.bitwise_and(i + step, CAP - 1)
-                value = jnp.sum(left * res_ref[j, :, span], axis=0, keepdims=True)
+                value = jnp.sum(left * res_ref[h, j], axis=0, keepdims=True)
                 gram_ref[h, i, pl.ds(j, 1), :] = value
                 gram_ref[h, j, pl.ds(i, 1), :] = value
         return carry
@@ -264,7 +283,7 @@
         tile = pl.ds(pl.multiple_of(t * 8, 8), 8)
         for h in range(LISTS // LANES):
             span = slice(h * LANES, (h + 1) * LANES)
-            parts = weave([res_ref[j, tile, span] for j in range(CAP)], lane[:8])
+            parts = weave([res_ref[h, j, tile, :] for j in range(CAP)], lane[:8])
             for j in range(CAP):
                 at = (h * CAP + j) * LANES
                 woven_ref[tile, at : at + LANES] = parts[j]
@@ -314,7 +333,7 @@
         scratch_shapes=[
             pltpu.VMEM((LISTS // LANES, CAP, CAP, LANES), f32),
             pltpu.VMEM((POWERS - 1, CAP, CAP, LANES), f32),
-            pltpu.VMEM((CAP + 1, D, LISTS), f32),
+            pltpu.VMEM((LISTS // LANES, CAP + 2, D, LANES), f32),
             pltpu.SemaphoreType.DMA,
         ],
         cost_estimate=pl.CostEstimate(flops=2 * CAP * CAP * D * LISTS, bytes_accessed=8 * CAP * D * LISTS, transcendentals=0),
@@ -416,11 +435,8 @@
         value = woven_ref[:D, span]
         high = value.astype(bf16)
         low = (value - high.astype(f32)).astype(bf16)
-        out_ref[:, span] = (
-            jnp.dot(high, coarse, preferred_element_type=f32)
-            + jnp.dot(low, coarse, preferred_element_type=f32)
-            + jnp.dot(high, fine, preferred_element_type=f32)
-        )
+        both = jnp.dot(jnp.concatenate([high, low], axis=0), coarse, preferred_element_type=f32)
+        out_ref[:, span] = both[:D] + both[D:] + jnp.dot(high, fine, preferred_element_type=f32)
         copies.append(pltpu.make_async_copy(out_ref.at[:, span], out_hbm.at[:, span], sem.at[g]))
         copies[g].start()
     for copy in copies:

time: 67.7 us -> 67 us (0.990)
  no operation moved by 1% of the time
where the time goes in v4:
time: 67 us; the launch traced here: 66.8 us
  blocking collectives  36.8 us (55%)
  Pallas kernels  23.8 us (36%)
  starting transfers between devices  4.63 us (7%)
  waiting for transfers between devices  0.85 us (1%)
  between operations  0.68 us (1%)
    all_to_all x1, blocking collectives, local(): lax.all_to_all(outgoing, AXES, split_axis=0, concat_axis=0, tiled=True)  36.8 us
    pallas_call x1, Pallas kernels, gram(): pl.pallas_call(gram_kernel, out_shape=(jax.ShapeDtypeStruct((D + POWERS *...  8.58 us
    pallas_call x1, Pallas kernels, place(): pl.pallas_call(place_kernel, out_shape=(pltpu.HBM((LISTS // LANES, CAP +...  6.06 us
    pallas_call x1, Pallas kernels, whiten(): pl.pallas_call(whiten_kernel, out_shape=jax.ShapeDtypeStruct((D, CELLS),...  4.75 us
    all_to_all x1, starting transfers between devices, local(): lax.all_to_all(energy.reshape(DEV, 1, LANES), AXES, split_axis=0, concat_...  4.63 us
    pallas_call x1, Pallas kernels, dispatch(): pl.pallas_call(dispatch_kernel, out_shape=jax.ShapeDtypeStruct((DEV * BLO...  4.41 us
  transfers between devices with their start and end apart: 1, of which 1 were waited for; matrix products, arithmetic and copies ran while one was open for 0% of the time, Pallas kernels for 13%

profile of v4, /device:TPU:1, one launch (start us, length us, event | category | flops | bytes accessed | tf_op | source)
XLA Modules:
  0.0 66.8 jit_solution(16782354237392285828)
XLA Ops:
  0.6 4.4 %dispatch.1 = f32[3200,128]{1,0:T(8,128)S(1)} custom-call(f32[96,2048]{1,0:T(8,128)} %vec_hbm.1, s32[16,128]{1,0:T(8,128)} %bitcast.13, s32[16,128]{1,0:T(8,128)} %bitcast.14), custom_call_target="tpu_custom_call" | custom-call | tf_op jit(solution)/shard_map/dispatch/pallas_call | solution.py:111
  5.0 0.0 copy-start
  5.1 0.0 copy-start.1
  5.1 36.8 %all_to_all.10 = f32[128,1,3200]{2,1,0:T(1,128)S(1)} all-to-all(f32[128,1,3200]{2,1,0:T(1,128)S(1)} %bitcast.10), channel_id=1, replica_groups=mesh['dp'=16,'owner'=8] {'dp','owner'}, dimensions={0} | all-to-all | bytes 3276800 | tf_op jit(solution)/shard_map/all_to_all | solution.py:467
  41.9 0.0 copy-done
  41.9 0.0 copy-done.1
  41.9 6.1 %place.1 = (f32[2,18,96,128]{3,2,1,0:T(8,128)}, f32[8,256]{1,0:T(8,128)S(1)}, f32[128,128]{1,0:T(8,128)}) custom-call(f32[3200,128]{1,0:T(8,128)S(1)} %bitcast.9, f32[96,256]{1,0:T(8,128)S(1)} %copy-done, s32[1,256]{1,0:T(1,128)S(1)} %bitcast.12), custom_call_target="tpu_custom_call" | custom-call | tf_op jit(solution)/shard_map/place/pallas_call | solution.py:213
  47.9 4.6 %all-to-all-start.1 = ((f32[128,1,128]{2,1,0:T(1,128)}), f32[128,1,128]{2,1,0:T(1,128)S(1)}, u32[]{:S(2)}, u32[]{:S(2)}) async-start(f32[128,1,128]{2,1,0:T(1,128)} %bitcast.6), calls=%async_computation.1 | async-start | bytes 131072 | tf_op jit(solution)/shard_map/all_to_all | solution.py:469
  52.6 8.6 %gram.1 = (f32[168,4096]{1,0:T(8,128)S(1)}, f32[96,256]{1,0:T(8,128)}) custom-call(f32[2,18,96,128]{3,2,1,0:T(8,128)} %get-tuple-element.7.res_hbm), custom_call_target="tpu_custom_call" | custom-call | flops 12582912 | bytes 3145728 | tf_op jit(solution)/shard_map/gram/pallas_call | solution.py:325
  61.2 0.9 %all-to-all-done.1 = f32[128,1,128]{2,1,0:T(1,128)S(1)} async-done(((f32[128,1,128]{2,1,0:T(1,128)}), f32[128,1,128]{2,1,0:T(1,128)S(1)}, u32[]{:S(2)}, u32[]{:S(2)}) %all-to-all-start.1) | async-done | bytes 65568 | tf_op jit(solution)/shard_map/all_to_all | solution.py:469
  62.0 4.7 %whiten.1 = f32[96,4096]{1,0:T(8,128)} custom-call(f32[168,4096]{1,0:T(8,128)S(1)} %get-tuple-element.9.woven_ref, f32[8,256]{1,0:T(8,128)S(1)} %get-tuple-element.10.stat_ref, f32[128,128]{1,0:T(8,128)S(1)} %bitcast.11), custom_call_target="tpu_custom_call" | custom-call | tf_op jit(solution)/shard_map/whiten/pallas_call | solution.py:448
Async XLA Ops:
  5.0 36.8 %copy-start = (f32[96,256]{1,0:T(8,128)S(1)}, f32[96,256]{1,0:T(8,128)}, u32[]{:S(2)}) copy-start(f32[96,256]{1,0:T(8,128)} %old_ref.1) | copy-start | bytes 294916
  5.1 36.8 %copy-start.1 = (s32[256]{0:T(256)S(1)}, s32[256]{0:T(256)}, u32[]{:S(2)}) copy-start(s32[256]{0:T(256)} %param.9) | copy-start | bytes 3076
  47.9 14.1 %all-to-all-start.1 = ((f32[128,1,128]{2,1,0:T(1,128)}), f32[128,1,128]{2,1,0:T(1,128)S(1)}, u32[]{:S(2)}, u32[]{:S(2)}) async-start(f32[128,1,128]{2,1,0:T(1,128)} %bitcast.6), calls=%async_computation.1 | async-start | bytes 131072 | tf_op jit(solution)/shard_map/all_to_all | solution.py:469

commit v5 on v4

--- a/solution.py
+++ b/solution.py
@@ -128,7 +128,7 @@
     )(*(pltpu.with_memory_space_constraint(x, pltpu.HBM) for x in arrays))
 
 
-def place_kernel(got_ref, old_ref, prior_ref, res_hbm, stat_ref, energy_ref, res_ref, cells, tails, lab_v, lab_s, sem, out_sem):
+def place_kernel(got_ref, old_ref, prior_ref, res_hbm, stat_ref, energy_hbm, energy_ref, res_ref, cells, tails, lab_v, lab_s, sem, out_sem):
     f32, i32 = jnp.float32, jnp.int32
     lab_v[...] = got_ref[pl.ds(MAIN, DEV, stride=BLOCK), :].astype(i32)
     copy = pltpu.make_async_copy(lab_v, lab_s, sem)
@@ -204,6 +204,8 @@
             for t in range(D // 8):
                 total = total + square[8 * t : 8 * t + 8]
     energy_ref[...] = jnp.broadcast_to(jnp.sum(total, axis=0, keepdims=True), (DEV, LANES))
+    outs.append(pltpu.make_async_copy(energy_ref, energy_hbm, out_sem.at[len(outs)]))
+    outs[-1].start()
     for out in outs:
         out.wait()
 
@@ -215,18 +217,19 @@
         out_shape=(
             pltpu.HBM((LISTS // LANES, CAP + 2, D, LANES), f32),
             jax.ShapeDtypeStruct((8, LISTS), f32),
-            jax.ShapeDtypeStruct((DEV, LANES), f32),
+            pltpu.HBM((DEV, LANES), f32),
         ),
         in_specs=[VMEM] * 3,
-        out_specs=(HBM, VMEM, VMEM),
+        out_specs=(HBM, VMEM, HBM),
         scratch_shapes=[
+            pltpu.VMEM((DEV, LANES), f32),
             pltpu.VMEM((LISTS // LANES, CAP + 2, D, LANES), f32),
             pltpu.VMEM((CELLS + 8, LANES), f32),
             pltpu.VMEM((DEV * (SEND - MAIN), LANES), f32),
             pltpu.VMEM((DEV, LANES), jnp.int32),
             pltpu.SMEM((DEV, LANES), jnp.int32),
             pltpu.SemaphoreType.DMA,
-            pltpu.SemaphoreType.DMA((10,)),
+            pltpu.SemaphoreType.DMA((11,)),
         ],
         compiler_params=pltpu.CompilerParams(vmem_limit_bytes=GRANT),
         name="place",

time: 67 us -> 66.5 us (level)
  no operation moved by 1% of the time
where the time goes in v5:
time: 66.5 us; the launch traced here: 66.2 us
  blocking collectives  36.8 us (55%)
  Pallas kernels  23.4 us (35%)
  starting transfers between devices  4.63 us (7%)
  waiting for transfers between devices  0.75 us (1%)
  between operations  0.68 us (1%)
    all_to_all x1, blocking collectives, local(): lax.all_to_all(outgoing, AXES, split_axis=0, concat_axis=0, tiled=True)  36.8 us
    pallas_call x1, Pallas kernels, gram(): pl.pallas_call(gram_kernel, out_shape=(jax.ShapeDtypeStruct((D + POWERS *...  8.68 us
    pallas_call x1, Pallas kernels, place(): pl.pallas_call(place_kernel, out_shape=(pltpu.HBM((LISTS // LANES, CAP +...  5.5 us
    pallas_call x1, Pallas kernels, whiten(): pl.pallas_call(whiten_kernel, out_shape=jax.ShapeDtypeStruct((D, CELLS),...  4.78 us
    all_to_all x1, starting transfers between devices, local(): lax.all_to_all(energy.reshape(DEV, 1, LANES), AXES, split_axis=0, concat_...  4.63 us
    pallas_call x1, Pallas kernels, dispatch(): pl.pallas_call(dispatch_kernel, out_shape=jax.ShapeDtypeStruct((DEV * BLO...  4.41 us
  transfers between devices with their start and end apart: 1, of which 1 were waited for; matrix products, arithmetic and copies ran while one was open for 0% of the time, Pallas kernels for 13%

profile of v5, /device:TPU:1, one launch (start us, length us, event | category | flops | bytes accessed | tf_op | source)
XLA Modules:
  0.0 66.2 jit_solution(7113046633877536589)
XLA Ops:
  0.6 4.4 %dispatch.1 = f32[3200,128]{1,0:T(8,128)S(1)} custom-call(f32[96,2048]{1,0:T(8,128)} %vec_hbm.1, s32[16,128]{1,0:T(8,128)} %bitcast.14, s32[16,128]{1,0:T(8,128)} %bitcast.15), custom_call_target="tpu_custom_call" | custom-call | tf_op jit(solution)/shard_map/dispatch/pallas_call | solution.py:111
  5.0 0.0 copy-start
  5.1 0.0 copy-start.1
  5.1 36.8 %all_to_all.10 = f32[128,1,3200]{2,1,0:T(1,128)S(1)} all-to-all(f32[128,1,3200]{2,1,0:T(1,128)S(1)} %bitcast.10), channel_id=1, replica_groups=mesh['dp'=16,'owner'=8] {'dp','owner'}, dimensions={0} | all-to-all | bytes 3276800 | tf_op jit(solution)/shard_map/all_to_all | solution.py:470
  41.9 0.0 copy-done
  41.9 0.0 copy-done.1
  41.9 5.5 %place.1 = (f32[2,18,96,128]{3,2,1,0:T(8,128)}, f32[8,256]{1,0:T(8,128)S(1)}, f32[128,128]{1,0:T(8,128)}) custom-call(f32[3200,128]{1,0:T(8,128)S(1)} %bitcast.9, f32[96,256]{1,0:T(8,128)S(1)} %copy-done, s32[1,256]{1,0:T(1,128)S(1)} %bitcast.12), custom_call_target="tpu_custom_call" | custom-call | tf_op jit(solution)/shard_map/place/pallas_call | solution.py:215
  47.4 4.6 %all-to-all-start.1 = ((f32[128,1,128]{2,1,0:T(1,128)}), f32[128,1,128]{2,1,0:T(1,128)S(1)}, u32[]{:S(2)}, u32[]{:S(2)}) async-start(f32[128,1,128]{2,1,0:T(1,128)} %bitcast.13), calls=%async_computation.1 | async-start | bytes 131072 | tf_op jit(solution)/shard_map/all_to_all | solution.py:472
  52.0 8.7 %gram.1 = (f32[168,4096]{1,0:T(8,128)S(1)}, f32[96,256]{1,0:T(8,128)}) custom-call(f32[2,18,96,128]{3,2,1,0:T(8,128)} %get-tuple-element.7.res_hbm), custom_call_target="tpu_custom_call" | custom-call | flops 12582912 | bytes 3145728 | tf_op jit(solution)/shard_map/gram/pallas_call | solution.py:328
  60.7 0.8 %all-to-all-done.1 = f32[128,1,128]{2,1,0:T(1,128)S(1)} async-done(((f32[128,1,128]{2,1,0:T(1,128)}), f32[128,1,128]{2,1,0:T(1,128)S(1)}, u32[]{:S(2)}, u32[]{:S(2)}) %all-to-all-start.1) | async-done | bytes 65568 | tf_op jit(solution)/shard_map/all_to_all | solution.py:472
  61.5 4.8 %whiten.1 = f32[96,4096]{1,0:T(8,128)} custom-call(f32[168,4096]{1,0:T(8,128)S(1)} %get-tuple-element.9.woven_ref, f32[8,256]{1,0:T(8,128)S(1)} %get-tuple-element.10.stat_ref, f32[128,128]{1,0:T(8,128)S(1)} %bitcast.11), custom_call_target="tpu_custom_call" | custom-call | tf_op jit(solution)/shard_map/whiten/pallas_call | solution.py:451
Async XLA Ops:
  5.0 36.8 %copy-start = (f32[96,256]{1,0:T(8,128)S(1)}, f32[96,256]{1,0:T(8,128)}, u32[]{:S(2)}) copy-start(f32[96,256]{1,0:T(8,128)} %old_ref.1) | copy-start | bytes 294916
  5.1 36.8 %copy-start.1 = (s32[256]{0:T(256)S(1)}, s32[256]{0:T(256)}, u32[]{:S(2)}) copy-start(s32[256]{0:T(256)} %param.9) | copy-start | bytes 3076
  47.4 14.1 %all-to-all-start.1 = ((f32[128,1,128]{2,1,0:T(1,128)}), f32[128,1,128]{2,1,0:T(1,128)S(1)}, u32[]{:S(2)}, u32[]{:S(2)}) async-start(f32[128,1,128]{2,1,0:T(1,128)} %bitcast.13), calls=%async_computation.1 | async-start | bytes 131072 | tf_op jit(solution)/shard_map/all_to_all | solution.py:472

commit v6 on v5

--- a/solution.py
+++ b/solution.py
@@ -14,6 +14,8 @@
 SEND = 32
 STEPS = 4
 AXES = ("dp", "owner")
+EXCHANGE = ("owner", "dp")
+OWNERS = 8
 LANES = 128
 TAIL = D - CAP
 MAIN = 24
@@ -41,7 +43,8 @@
     get_assign.wait()
     get_slot.wait()
     assign = assign_ref[...]
-    owner = lax.shift_right_logical(assign, 8)
+    device = lax.shift_right_logical(assign, 8)
+    owner = jnp.bitwise_and(device, OWNERS - 1) * (DEV // OWNERS) + lax.shift_right_logical(device, 3)
     here = jnp.bitwise_and(assign, LISTS - 1)
     half = jnp.bitwise_and(here, LANES - 1)
     lane = jnp.bitwise_and(here, LANES) + jnp.bitwise_and(half, 7) * 16 + lax.shift_right_logical(half, 3)
@@ -467,9 +470,9 @@
 
 def local(vectors, assignment, slot, old_centroids, prior_counts):
     outgoing = dispatch(vectors, assignment, slot).reshape(DEV, 1, BLOCK * LANES)
-    incoming = lax.all_to_all(outgoing, AXES, split_axis=0, concat_axis=0, tiled=True)
+    incoming = lax.all_to_all(outgoing, EXCHANGE, split_axis=0, concat_axis=0, tiled=True)
     res, stat, energy = place(incoming.reshape(DEV * BLOCK, LANES), old_centroids, prior_counts)
-    shared = lax.all_to_all(energy.reshape(DEV, 1, LANES), AXES, split_axis=0, concat_axis=0, tiled=True)
+    shared = lax.all_to_all(energy.reshape(DEV, 1, LANES), EXCHANGE, split_axis=0, concat_axis=0, tiled=True)
     woven, centroids = gram(res)
     rotated = whiten(woven, stat, shared.reshape(DEV, LANES))
     return (centroids, rotated)

time: 66.5 us -> 66.2 us (level)
  blocking collectives: 36.8 us -> 36.1 us
    all_to_all x1, blocking collectives: 36.8 us -> 36.1 us  [local(): lax.all_to_all(outgoing, EXCHANGE, split_axis=0, concat_axis=0, tiled=True)]
where the time goes in v6:
time: 66.2 us; the launch traced here: 65.9 us
  blocking collectives  36.1 us (55%)
  Pallas kernels  23.4 us (35%)
  starting transfers between devices  4.79 us (7%)
  waiting for transfers between devices  0.98 us (1%)
  between operations  0.68 us (1%)
    all_to_all x1, blocking collectives, local(): lax.all_to_all(outgoing, EXCHANGE, split_axis=0, concat_axis=0, tiled=True)  36.1 us
    pallas_call x1, Pallas kernels, gram(): pl.pallas_call(gram_kernel, out_shape=(jax.ShapeDtypeStruct((D + POWERS *...  8.68 us
    pallas_call x1, Pallas kernels, place(): pl.pallas_call(place_kernel, out_shape=(pltpu.HBM((LISTS // LANES, CAP +...  5.5 us
    all_to_all x1, starting transfers between devices, local(): lax.all_to_all(energy.reshape(DEV, 1, LANES), EXCHANGE, split_axis=0, con...  4.79 us
    pallas_call x1, Pallas kernels, whiten(): pl.pallas_call(whiten_kernel, out_shape=jax.ShapeDtypeStruct((D, CELLS),...  4.78 us
    pallas_call x1, Pallas kernels, dispatch(): pl.pallas_call(dispatch_kernel, out_shape=jax.ShapeDtypeStruct((DEV * BLO...  4.41 us
  transfers between devices with their start and end apart: 1, of which 1 were waited for; matrix products, arithmetic and copies ran while one was open for 0% of the time, Pallas kernels for 13%

profile of v6, /device:TPU:1, one launch (start us, length us, event | category | flops | bytes accessed | tf_op | source)
XLA Modules:
  0.0 65.9 jit_solution(17210378984206834011)
XLA Ops:
  0.6 4.4 %dispatch.1 = f32[3200,128]{1,0:T(8,128)S(1)} custom-call(f32[96,2048]{1,0:T(8,128)} %vec_hbm.1, s32[16,128]{1,0:T(8,128)} %bitcast.14, s32[16,128]{1,0:T(8,128)} %bitcast.15), custom_call_target="tpu_custom_call" | custom-call | tf_op jit(solution)/shard_map/dispatch/pallas_call | solution.py:114
  5.0 0.0 copy-start
  5.1 0.0 copy-start.1
  5.1 36.1 %all_to_all.10 = f32[128,1,3200]{2,1,0:T(1,128)S(1)} all-to-all(f32[128,1,3200]{2,1,0:T(1,128)S(1)} %bitcast.10), channel_id=1, replica_groups=mesh['dp'=16,'owner'=8] {'owner','dp'}, dimensions={0} | all-to-all | bytes 3276800 | tf_op jit(solution)/shard_map/all_to_all | solution.py:473
  41.2 0.0 copy-done
  41.2 0.0 copy-done.1
  41.2 5.5 %place.1 = (f32[2,18,96,128]{3,2,1,0:T(8,128)}, f32[8,256]{1,0:T(8,128)S(1)}, f32[128,128]{1,0:T(8,128)}) custom-call(f32[3200,128]{1,0:T(8,128)S(1)} %bitcast.9, f32[96,256]{1,0:T(8,128)S(1)} %copy-done, s32[1,256]{1,0:T(1,128)S(1)} %bitcast.12), custom_call_target="tpu_custom_call" | custom-call | tf_op jit(solution)/shard_map/place/pallas_call | solution.py:218
  46.7 4.8 %all-to-all-start.1 = ((f32[128,1,128]{2,1,0:T(1,128)}), f32[128,1,128]{2,1,0:T(1,128)S(1)}, u32[]{:S(2)}, u32[]{:S(2)}) async-start(f32[128,1,128]{2,1,0:T(1,128)} %bitcast.13), calls=%async_computation.1 | async-start | bytes 131072 | tf_op jit(solution)/shard_map/all_to_all | solution.py:475
  51.5 8.7 %gram.1 = (f32[168,4096]{1,0:T(8,128)S(1)}, f32[96,256]{1,0:T(8,128)}) custom-call(f32[2,18,96,128]{3,2,1,0:T(8,128)} %get-tuple-element.7.res_hbm), custom_call_target="tpu_custom_call" | custom-call | flops 12582912 | bytes 3145728 | tf_op jit(solution)/shard_map/gram/pallas_call | solution.py:331
  60.2 1.0 %all-to-all-done.1 = f32[128,1,128]{2,1,0:T(1,128)S(1)} async-done(((f32[128,1,128]{2,1,0:T(1,128)}), f32[128,1,128]{2,1,0:T(1,128)S(1)}, u32[]{:S(2)}, u32[]{:S(2)}) %all-to-all-start.1) | async-done | bytes 65568 | tf_op jit(solution)/shard_map/all_to_all | solution.py:475
  61.2 4.8 %whiten.1 = f32[96,4096]{1,0:T(8,128)} custom-call(f32[168,4096]{1,0:T(8,128)S(1)} %get-tuple-element.9.woven_ref, f32[8,256]{1,0:T(8,128)S(1)} %get-tuple-element.10.stat_ref, f32[128,128]{1,0:T(8,128)S(1)} %bitcast.11), custom_call_target="tpu_custom_call" | custom-call | tf_op jit(solution)/shard_map/whiten/pallas_call | solution.py:454
Async XLA Ops:
  5.0 36.1 %copy-start = (f32[96,256]{1,0:T(8,128)S(1)}, f32[96,256]{1,0:T(8,128)}, u32[]{:S(2)}) copy-start(f32[96,256]{1,0:T(8,128)} %old_ref.1) | copy-start | bytes 294916
  5.1 36.1 %copy-start.1 = (s32[256]{0:T(256)S(1)}, s32[256]{0:T(256)}, u32[]{:S(2)}) copy-start(s32[256]{0:T(256)} %param.9) | copy-start | bytes 3076
  46.7 14.5 %all-to-all-start.1 = ((f32[128,1,128]{2,1,0:T(1,128)}), f32[128,1,128]{2,1,0:T(1,128)S(1)}, u32[]{:S(2)}, u32[]{:S(2)}) async-start(f32[128,1,128]{2,1,0:T(1,128)} %bitcast.13), calls=%async_computation.1 | async-start | bytes 131072 | tf_op jit(solution)/shard_map/all_to_all | solution.py:475

commit v7 on v5

--- a/solution.py
+++ b/solution.py
@@ -160,7 +160,7 @@
     total = jnp.zeros((8, LANES), f32)
     outs = []
     gathered = []
-    part = 4
+    part = 2
 
     def send(h, planes):
         outs.append(
@@ -229,7 +229,7 @@
             pltpu.VMEM((DEV, LANES), jnp.int32),
             pltpu.SMEM((DEV, LANES), jnp.int32),
             pltpu.SemaphoreType.DMA,
-            pltpu.SemaphoreType.DMA((11,)),
+            pltpu.SemaphoreType.DMA((19,)),
         ],
         compiler_params=pltpu.CompilerParams(vmem_limit_bytes=GRANT),
         name="place",

time: 66.5 us -> 66.5 us (level)
  no operation moved by 1% of the time
where the time goes in v7:
time: 66.5 us; the launch traced here: 66.3 us
  blocking collectives  36.8 us (55%)
  Pallas kernels  23.4 us (35%)
  starting transfers between devices  4.63 us (7%)
  waiting for transfers between devices  0.75 us (1%)
  between operations  0.68 us (1%)
    all_to_all x1, blocking collectives, local(): lax.all_to_all(outgoing, AXES, split_axis=0, concat_axis=0, tiled=True)  36.8 us
    pallas_call x1, Pallas kernels, gram(): pl.pallas_call(gram_kernel, out_shape=(jax.ShapeDtypeStruct((D + POWERS *...  8.68 us
    pallas_call x1, Pallas kernels, place(): pl.pallas_call(place_kernel, out_shape=(pltpu.HBM((LISTS // LANES, CAP +...  5.57 us
    pallas_call x1, Pallas kernels, whiten(): pl.pallas_call(whiten_kernel, out_shape=jax.ShapeDtypeStruct((D, CELLS),...  4.78 us
    all_to_all x1, starting transfers between devices, local(): lax.all_to_all(energy.reshape(DEV, 1, LANES), AXES, split_axis=0, concat_...  4.63 us
    pallas_call x1, Pallas kernels, dispatch(): pl.pallas_call(dispatch_kernel, out_shape=jax.ShapeDtypeStruct((DEV * BLO...  4.41 us
  transfers between devices with their start and end apart: 1, of which 1 were waited for; matrix products, arithmetic and copies ran while one was open for 0% of the time, Pallas kernels for 13%

profile of v7, /device:TPU:1, one launch (start us, length us, event | category | flops | bytes accessed | tf_op | source)
XLA Modules:
  0.0 66.3 jit_solution(3966981107422745845)
XLA Ops:
  0.6 4.4 %dispatch.1 = f32[3200,128]{1,0:T(8,128)S(1)} custom-call(f32[96,2048]{1,0:T(8,128)} %vec_hbm.1, s32[16,128]{1,0:T(8,128)} %bitcast.14, s32[16,128]{1,0:T(8,128)} %bitcast.15), custom_call_target="tpu_custom_call" | custom-call | tf_op jit(solution)/shard_map/dispatch/pallas_call | solution.py:111
  5.0 0.0 copy-start
  5.1 0.0 copy-start.1
  5.1 36.8 %all_to_all.10 = f32[128,1,3200]{2,1,0:T(1,128)S(1)} all-to-all(f32[128,1,3200]{2,1,0:T(1,128)S(1)} %bitcast.10), channel_id=1, replica_groups=mesh['dp'=16,'owner'=8] {'dp','owner'}, dimensions={0} | all-to-all | bytes 3276800 | tf_op jit(solution)/shard_map/all_to_all | solution.py:470
  41.9 0.0 copy-done
  41.9 0.0 copy-done.1
  41.9 5.6 %place.1 = (f32[2,18,96,128]{3,2,1,0:T(8,128)}, f32[8,256]{1,0:T(8,128)S(1)}, f32[128,128]{1,0:T(8,128)}) custom-call(f32[3200,128]{1,0:T(8,128)S(1)} %bitcast.9, f32[96,256]{1,0:T(8,128)S(1)} %copy-done, s32[1,256]{1,0:T(1,128)S(1)} %bitcast.12), custom_call_target="tpu_custom_call" | custom-call | tf_op jit(solution)/shard_map/place/pallas_call | solution.py:215
  47.5 4.6 %all-to-all-start.1 = ((f32[128,1,128]{2,1,0:T(1,128)}), f32[128,1,128]{2,1,0:T(1,128)S(1)}, u32[]{:S(2)}, u32[]{:S(2)}) async-start(f32[128,1,128]{2,1,0:T(1,128)} %bitcast.13), calls=%async_computation.1 | async-start | bytes 131072 | tf_op jit(solution)/shard_map/all_to_all | solution.py:472
  52.1 8.7 %gram.1 = (f32[168,4096]{1,0:T(8,128)S(1)}, f32[96,256]{1,0:T(8,128)}) custom-call(f32[2,18,96,128]{3,2,1,0:T(8,128)} %get-tuple-element.7.res_hbm), custom_call_target="tpu_custom_call" | custom-call | flops 12582912 | bytes 3145728 | tf_op jit(solution)/shard_map/gram/pallas_call | solution.py:328
  60.8 0.8 %all-to-all-done.1 = f32[128,1,128]{2,1,0:T(1,128)S(1)} async-done(((f32[128,1,128]{2,1,0:T(1,128)}), f32[128,1,128]{2,1,0:T(1,128)S(1)}, u32[]{:S(2)}, u32[]{:S(2)}) %all-to-all-start.1) | async-done | bytes 65568 | tf_op jit(solution)/shard_map/all_to_all | solution.py:472
  61.5 4.8 %whiten.1 = f32[96,4096]{1,0:T(8,128)} custom-call(f32[168,4096]{1,0:T(8,128)S(1)} %get-tuple-element.9.woven_ref, f32[8,256]{1,0:T(8,128)S(1)} %get-tuple-element.10.stat_ref, f32[128,128]{1,0:T(8,128)S(1)} %bitcast.11), custom_call_target="tpu_custom_call" | custom-call | tf_op jit(solution)/shard_map/whiten/pallas_call | solution.py:451
Async XLA Ops:
  5.0 36.8 %copy-start = (f32[96,256]{1,0:T(8,128)S(1)}, f32[96,256]{1,0:T(8,128)}, u32[]{:S(2)}) copy-start(f32[96,256]{1,0:T(8,128)} %old_ref.1) | copy-start | bytes 294916
  5.1 36.8 %copy-start.1 = (s32[256]{0:T(256)S(1)}, s32[256]{0:T(256)}, u32[]{:S(2)}) copy-start(s32[256]{0:T(256)} %param.9) | copy-start | bytes 3076
  47.5 14.1 %all-to-all-start.1 = ((f32[128,1,128]{2,1,0:T(1,128)}), f32[128,1,128]{2,1,0:T(1,128)S(1)}, u32[]{:S(2)}, u32[]{:S(2)}) async-start(f32[128,1,128]{2,1,0:T(1,128)} %bitcast.13), calls=%async_computation.1 | async-start | bytes 131072 | tf_op jit(solution)/shard_map/all_to_all | solution.py:472
